TPU v7x, 32 devices: a whole 2x2x4 slice. The times are simulated.
32 devices in a mesh: groups: 2 (over y), seq: 16 (over z, x, core).
Axes of the slice: x: 2, y: 2, z: 4, core: 2. Of those that a mesh axis runs over, the one named last changes fastest.
Arguments:
- pool_kv: bfloat16 [3072, 1024], P(('groups', 'seq')), parts along dimension 0, may hold values from -6 to 6
- pool_slot: int32 [32], P('groups'), parts along dimension 0, may hold values from 0 to 15, each once
- passage_order: int32 [32], P('groups'), parts along dimension 0, may hold values from 0 to 15, each once
- passage_start: int32 [32], P('groups'), parts along dimension 0, may hold values from 0 to 6784, as said below
- recompute_pos: int32 [32, 56], P('groups'), parts along dimension 0, may hold values from 0 to 383, as said below
- page_table: int32 [3072], P('groups'), parts along dimension 0, may hold values from 0 to 1535, as said below
- fresh_q: bfloat16 [1792, 1024], P(('groups', 'seq')), parts along dimension 0, may hold values from -64 to 64
- fresh_kv: bfloat16 [1792, 256], P(('groups', 'seq')), parts along dimension 0, may hold values from -64 to 64
Outputs:
- attended: bfloat16 [1792, 1024], P(('groups', 'seq')), parts along dimension 0
- decode_cache: bfloat16 [3072, 1024], P(('groups', 'seq')), parts along dimension 0
There are 2 independent parts, one for each index of `groups`. A program takes and returns all parts, laid end to end along the dimension named above; each array names one. Nothing has to cross between parts.
Inputs may be any that keep to these rules, and one draw needn't show every extreme that they name: `passage_start`: increases by at least 384 from one passage to the next; the first is 0 and the last is (15) * 384 + 1024. `recompute_pos`: each row holds 56 different positions of its passage in increasing order. `page_table`: every row of the decode cache receives exactly one page; of the 96 pages of one passage at most 6 go to the 96 rows of one owner, and that many do for some owner.
All inputs are finite; a program needn't handle non-finite values.
Results may differ from a plain program's by a relative error of at most 0.0075.
The roundings to bfloat16 on the way count: a program that leaves them out, or rounds other values in their place, can miss the bound.
Values may be sent and summed in bfloat16 or wider, within the bound.
A program may use at most 256 MiB of HBM per device.

v0:
```python
from functools import partial

import jax
import jax.numpy as jnp
from jax import lax
from jax.sharding import PartitionSpec as P

GROUP = 8
PAGE = 4


ROPE_BASE = 500000.0


def rotate_pos(vector, positions):
    half_dim = vector.shape[-1] // 2
    frequency = ROPE_BASE ** (-(jnp.arange(half_dim, dtype=jnp.float32) * (2.0 / vector.shape[-1])))
    angles = positions.astype(jnp.float32)[..., None] * frequency
    cosine = jnp.cos(angles)
    sine = jnp.sin(angles)
    lower_half = vector[..., :half_dim]
    upper_half = vector[..., half_dim:]
    return jnp.concatenate(
        [lower_half * cosine - upper_half * sine, upper_half * cosine + lower_half * sine], axis=-1
    )


def attend(running, query_rows, query_pos, key_part, value_part, key_pos, usable):
    peak_score, weight_sum, weighted = running
    score_scale = key_part.shape[1] ** (-0.5)
    scores = jnp.dot(query_rows, key_part.T, preferred_element_type=jnp.float32) * score_scale
    allowed = key_pos[None, :] <= query_pos[:, None]
    new_peak = jnp.maximum(peak_score, jnp.max(jnp.where(allowed, scores, -jnp.inf), axis=1))
    weights = jnp.where(allowed, jnp.exp(scores - new_peak[:, None]), 0.0)
    weight_sum = jnp.sum(weights, axis=1)
    weighted = jnp.dot(weights.astype(jnp.bfloat16), value_part, preferred_element_type=jnp.float32)
    return (new_peak, weight_sum, weighted)


def visit(running, prepared, key_part, value_part, key_pos):
    result = []
    for (query_rows, query_pos), group_state in zip(prepared, running):
        advance = partial(
            attend,
            query_rows=query_rows,
            query_pos=query_pos,
            key_part=key_part,
            value_part=value_part,
            key_pos=key_pos,
            usable=None,
        )
        group_state = advance(group_state)
        result.append(group_state)
    return tuple(result)


def shards(
    pool_kv, pool_slot, passage_order, passage_start, recompute_pos, page_table, fresh_q, fresh_kv
):
    seq_count = lax.axis_size("seq")
    my_index = lax.axis_index("seq")
    page_count = pool_kv.shape[0]
    row_width = pool_kv.shape[1]
    head_dim = fresh_kv.shape[1] // 2
    sel_count = fresh_q.shape[0]
    tok_count = page_count * PAGE
    capacity = max(1, page_count // seq_count)
    passage_ids = jnp.arange(seq_count, dtype=jnp.int32)
    page_ids = jnp.arange(page_count, dtype=jnp.int32)
    slot_holder = jnp.zeros((seq_count,), jnp.int32).at[pool_slot].set(passage_ids)
    passage_place = jnp.zeros((seq_count,), jnp.int32).at[passage_order].set(passage_ids)
    held_spot = page_ids * seq_count + my_index
    receiver = passage_place[slot_holder[held_spot // page_count]]
    outgoing = (
        jnp.zeros((seq_count * capacity, row_width), pool_kv.dtype)
        .at[receiver * capacity + page_ids % capacity]
        .set(pool_kv)
    )
    arrived = lax.all_to_all(outgoing, "seq", split_axis=0, concat_axis=0, tiled=True)
    wanted = pool_slot[passage_order[my_index]] * page_count + page_ids
    cached = arrived[wanted % seq_count * capacity + wanted // seq_count % capacity].reshape(
        tok_count, 2, head_dim
    )
    start_pos = passage_start[my_index]
    picked = recompute_pos[my_index]
    fresh_pos = start_pos + picked
    shifted = rotate_pos(
        cached[:, 0, :].astype(jnp.float32), jnp.broadcast_to(start_pos, (tok_count,))
    )
    fresh_keys = rotate_pos(fresh_kv[:, :head_dim].astype(jnp.float32), fresh_pos).astype(
        jnp.bfloat16
    )
    key_rows = shifted.astype(jnp.bfloat16).at[picked].set(fresh_keys)
    value_rows = cached[:, 1, :].at[picked].set(fresh_kv[:, head_dim:])
    blended = jnp.stack([key_rows, value_rows], axis=1)
    page_rows = blended.reshape(page_count, row_width)
    my_table = lax.dynamic_slice_in_dim(page_table, my_index * page_count, page_count)
    owners = my_table // page_count
    before = page_ids[None, :] < page_ids[:, None]
    rank_out = jnp.sum(jnp.logical_and(owners[None, :] == owners[:, None], before), axis=1)
    outgoing_pages = (
        jnp.zeros((seq_count * capacity, row_width), page_rows.dtype)
        .at[owners * capacity + rank_out]
        .set(page_rows)
    )
    landed = lax.all_to_all(outgoing_pages, "seq", split_axis=0, concat_axis=0, tiled=True)
    total_pages = seq_count * page_count
    page_source = (
        jnp.zeros((total_pages,), jnp.int32)
        .at[page_table]
        .set(jnp.arange(total_pages, dtype=jnp.int32))
    )
    my_sources = lax.dynamic_slice_in_dim(page_source, my_index * page_count, page_count)
    source_dev = my_sources // page_count
    source_page = my_sources % page_count
    source_owners = (page_table // page_count).reshape(seq_count, page_count)[source_dev]
    rank_in = jnp.sum(
        jnp.logical_and(source_owners == my_index, page_ids[None, :] < source_page[:, None]), axis=1
    )
    decode_cache = landed[source_dev * capacity + rank_in]
    queries = rotate_pos(
        fresh_q.reshape(sel_count, GROUP, head_dim).astype(jnp.float32), fresh_pos[:, None]
    ).astype(jnp.bfloat16)
    query_pos = my_index * tok_count + picked
    groups = [(queries, query_pos)]
    prepared = [
        (group_rows.reshape(-1, head_dim), jnp.repeat(positions, GROUP))
        for group_rows, positions in groups
    ]
    initial = []
    for group_rows, positions in prepared:
        row_count = group_rows.shape[0]
        initial.append(
            (
                jnp.full((row_count,), -1e30, jnp.float32),
                jnp.zeros((row_count,), jnp.float32),
                jnp.zeros((row_count, head_dim), jnp.float32),
            )
        )
    initial = tuple(initial)
    flat_rows = blended.reshape(tok_count, 2 * head_dim)
    piece = lax.all_gather(flat_rows, "seq", axis=0, tiled=True)
    key_pos = jnp.arange(piece.shape[0], dtype=jnp.int32)
    finals = visit(initial, prepared, piece[:, :head_dim], piece[:, head_dim:], key_pos)
    outputs = []
    for group_state in finals:
        outputs.append((group_state[2] / group_state[1][:, None]).astype(jnp.bfloat16))
    attended = outputs[0].reshape(sel_count, GROUP * head_dim)
    return (attended, decode_cache)


def solution(mesh):
    placed = (
        P(("groups", "seq"), None),
        P("groups"),
        P("groups"),
        P("groups"),
        P("groups", None),
        P("groups"),
        P(("groups", "seq"), None),
        P(("groups", "seq"), None),
    )
    return jax.shard_map(
        shards,
        mesh=mesh,
        in_specs=placed,
        out_specs=(P(("groups", "seq"), None), P(("groups", "seq"), None)),
        check_vma=False,
    )
```

profile of v0, /device:TPU:0, one launch (start us, length us, event | category | flops | bytes accessed | tf_op | source)
XLA Modules:
  0.0 124.0 jit_solution(2867619107465769491)
XLA Ops:
  7.2 0.7 compare_select_fusion.9
  7.8 0.7 compare_select_fusion.10
  9.1 0.7 fusion.58
  10.5 0.7 fusion.57
  11.2 20.1 %fusion.46 = s32[96]{0:T(128)S(1)} fusion(s32[]{:T(128)} %bitcast.50, s32[]{:T(128)} %bitcast.23, s32[]{:T(128)} %bitcast.51, s32[]{:T(128)} %bitcast.24, s32[]{:T(128)} %bitcast.52, s32[]{:T(128)} %bitcast.25, s32[]{:T(128)} %bitcast.53, s32[]{:T(128)} %bitcast.26, s32[]{:T(128)} %bitcast.54, s32[]{:T(128)} %bitcast.27, s32[]{:T(128)} %bitcast.56, ...), kind=kLoop, calls=%fused_computation.127 | loop fusion | flops 8352 | bytes 516 | tf_op jit(solution)/shard_map/select_n | solution.py:77
  31.3 1.4 %scatter_custom_fusion.2 = bf16[96,1024]{1,0:T(8,128)(2,1)S(1)} fusion(s32[96]{0:T(128)S(1)} %fusion.46, bf16[96,1024]{1,0:T(8,128)(2,1)} %param.8, bf16[]{:T(256)} %constant.84.clone.1), kind=kCustom, calls=%fused_computation.38 | custom fusion | bytes 197120 | tf_op jit(solution)/shard_map/scatter | solution.py:77
  32.7 0.8 all_to_all.16
  33.5 7.4 %all-to-all-start = ((bf16[16,6,1024]{2,1,0:T(8,128)(2,1)}), bf16[16,6,1024]{2,1,0:T(8,128)(2,1)S(1)}, u32[]{:S(2)}, u32[]{:S(2)}) async-start(bf16[16,6,1024]{2,1,0:T(8,128)(2,1)} %all_to_all.16), calls=%async_computation | async-start | bytes 524288 | tf_op jit(solution)/shard_map/all_to_all | solution.py:79
  40.9 1.2 %dynamic_slice.20 = s32[1]{0:T(128)} dynamic-slice(s32[16]{0:T(128)} %param.10, s32[]{:T(128)S(6)} %select_n.161), dynamic_slice_sizes={1} | dynamic-slice | bytes 12 | tf_op jit(solution)/shard_map/dynamic_slice | solution.py:80
  44.2 1.2 %dynamic_slice.21 = s32[1]{0:T(128)} dynamic-slice(s32[16]{0:T(128)} %param.9, s32[]{:T(128)S(6)} %select_n.169), dynamic_slice_sizes={1} | dynamic-slice | bytes 12 | tf_op jit(solution)/shard_map/dynamic_slice | solution.py:80
  45.4 1.2 dynamic_slice.19
  47.3 0.7 fusion.48
  48.0 1.3 %add_bitcast_fusion = (s32[56]{0:T(128)S(1)}, f32[56]{0:T(128)S(1)}) fusion(s32[]{:T(128)S(6)} %mul.169, s32[16,56]{1,0:T(8,128)} %param.12, s32[]{:T(128)S(6)} %select_n.161, s32[]{:T(128)} %bitcast.1), kind=kLoop, calls=%fused_computation.132 | loop fusion | flops 168 | bytes 684 | tf_op jit(solution)/shard_map/add | solution.py:124
  49.4 0.7 slice_convert_fusion
  51.1 0.8 gather_fusion
  52.3 1.0 scatter_custom_fusion.4
  53.5 0.9 scatter_custom_fusion.3
  54.5 0.8 copy.17
  55.3 0.7 compare_select_fusion
  56.1 6.2 %scatter_custom_fusion.6 = s32[1536]{0:T(1024)S(1)} fusion(s32[1536]{0:T(1024)S(1)} %get-tuple-element.13, s32[1536]{0:T(1024)S(1)} %iota.45, s32[]{:T(128)} %constant.80.clone.1), kind=kCustom, calls=%fused_computation.65 | custom fusion | bytes 6148 | tf_op jit(solution)/shard_map/scatter | solution.py:111
  62.3 0.8 compare_select_fusion.2
  64.1 0.9 convert_bitcast_fusion
  65.4 1.1 scatter_custom_fusion.5
  66.4 0.8 all_to_all.19
  67.2 6.0 %all-to-all-start.1 = ((bf16[16,6,1024]{2,1,0:T(8,128)(2,1)}), bf16[16,6,1024]{2,1,0:T(8,128)(2,1)S(1)}, u32[]{:S(2)}, u32[]{:S(2)}) async-start(bf16[16,6,1024]{2,1,0:T(8,128)(2,1)} %all_to_all.19), calls=%async_computation.1 | async-start | bytes 524288 | tf_op jit(solution)/shard_map/all_to_all | solution.py:106
  73.6 10.1 %all-to-all-done.1 = bf16[16,6,1024]{2,1,0:T(8,128)(2,1)S(1)} async-done(((bf16[16,6,1024]{2,1,0:T(8,128)(2,1)}), bf16[16,6,1024]{2,1,0:T(8,128)(2,1)S(1)}, u32[]{:S(2)}, u32[]{:S(2)}) %all-to-all-start.1) | async-done | bytes 196640 | tf_op jit(solution)/shard_map/all_to_all | solution.py:106
  83.8 1.5 %gather_fusion.2 = bf16[96,1024]{1,0:T(8,128)(2,1)} fusion(bf16[96,1024]{1,0:T(8,128)(2,1)S(1)} %all_to_all.21, s32[1024]{0:T(1024)S(1)} %pad_clamp_fusion), kind=kCustom, calls=%fused_computation.2 | custom fusion | bytes 393600 | tf_op jit(solution)/shard_map/gather | solution.py:120
  85.2 21.7 %all-gather.2.cloned.1.call-done = bf16[6144,256]{0,1:T(8,128)(2,1)} async-done(((bf16[384,256]{0,1:T(8,128)(2,1)}), bf16[6144,256]{0,1:T(8,128)(2,1)}) %all-gather.2.cloned.1.call-update) | async-done | bytes 3145744 | tf_op jit(solution)/shard_map/all_gather | solution.py:142
  107.0 3.9 %select_reduce_fusion = (f32[448]{0:T(512)S(1)}, f32[448,6144]{1,0:T(8,128)S(1)}) fusion(s32[448]{0:T(512)S(1)} %le.16, bf16[6144,256]{0,1:T(8,128)(2,1)} %all-gather.2.cloned.1.call-done, bf16[448,64]{1,0:T(8,128)(2,1)S(1)} %get-tuple-element.5, bf16[448,64]{1,0:T(8,128)(2,1)S(1)} %get-tuple-element.4), kind=kOutput, calls=%fused_computation.11 | convolution fusion | flops 715882048 | bytes 12701184 | tf_op jit(solution)/shard_map/dot_general | solution.py:31
  110.8 3.0 %fusion = f32[448]{0:T(512)S(1)} fusion(f32[448,6144]{1,0:T(8,128)S(1)} %get-tuple-element.52, f32[448]{0:T(512)S(1)} %broadcast_maximum_fusion, s32[448]{0:T(512)S(1)} %le.16), kind=kLoop, calls=%fused_computation.13 | loop fusion | flops 13762112 | bytes 11015424 | tf_op jit(solution)/shard_map/reduce_sum | solution.py:35
  113.8 2.6 %fusion.12 = bf16[448,128]{1,0:T(8,128)(2,1)S(1)} fusion(bf16[6144,256]{0,1:T(8,128)(2,1)S(1)} %copy-done, f32[448,6144]{1,0:T(8,128)S(1)} %get-tuple-element.52, f32[448]{0:T(512)S(1)} %broadcast_maximum_fusion, s32[448]{0:T(512)S(1)} %le.16, f32[448]{0:T(512)S(1)} %fusion), kind=kOutput, calls=%fused_computation.20 | convolution fusion | flops 718520320 | bytes 12703744 | tf_op jit(solution)/shard_map/dot_general | solution.py:36
  116.5 0.7 reshape.365
  (38 shorter events, 4.2 us)
Async XLA Ops:
  33.5 17.5 %all-to-all-start = ((bf16[16,6,1024]{2,1,0:T(8,128)(2,1)}), bf16[16,6,1024]{2,1,0:T(8,128)(2,1)S(1)}, u32[]{:S(2)}, u32[]{:S(2)}) async-start(bf16[16,6,1024]{2,1,0:T(8,128)(2,1)} %all_to_all.16), calls=%async_computation | async-start | bytes 524288 | tf_op jit(solution)/shard_map/all_to_all | solution.py:79
  40.9 66.1 %all-gather.2.cloned.1.call-start = ((), (), s32[]{:S(2)}) async-start(), calls=%async_computation.2 | async-start | bytes 3342336 | tf_op jit(solution)/shard_map/all_gather | solution.py:142
  67.2 16.5 %all-to-all-start.1 = ((bf16[16,6,1024]{2,1,0:T(8,128)(2,1)}), bf16[16,6,1024]{2,1,0:T(8,128)(2,1)S(1)}, u32[]{:S(2)}, u32[]{:S(2)}) async-start(bf16[16,6,1024]{2,1,0:T(8,128)(2,1)} %all_to_all.19), calls=%async_computation.1 | async-start | bytes 524288 | tf_op jit(solution)/shard_map/all_to_all | solution.py:106
  107.0 6.9 %copy-start = (bf16[6144,256]{0,1:T(8,128)(2,1)S(1)}, bf16[6144,256]{0,1:T(8,128)(2,1)}, u32[]{:S(2)}) copy-start(bf16[6144,256]{0,1:T(8,128)(2,1)} %all-gather.2.cloned.1.call-done) | copy-start | bytes 9437188
Sparse Core Ops, SparseCore 0:
  55.5 51.4 all-gather.1
where the time goes:
time: 125 us; the launch traced here: 124 us
  waiting for transfers between devices  31.8 us (25%)
  other arithmetic  31.6 us (25%)
  local copies, waits for them, and re-layouts  23.2 us (19%)
  between operations  17.5 us (14%)
  starting transfers between devices  13.4 us (11%)
  matrix products  6.5 us (5%)
    all_gather x1, waiting for transfers between devices, shards(): piece = lax.all_gather(flat_rows, 'seq', axis=0, tiled=True)  21.7 us
    select_n x1, other arithmetic, shards(): outgoing = jnp.zeros((seq_count * capacity, row_width), pool_kv.dtype).at...  20.1 us
    all_to_all x1, waiting for transfers between devices, shards(): lax.all_to_all(outgoing_pages, 'seq', split_axis=0, concat_axis=0, tiled=...  10.1 us
    all_to_all x1, starting transfers between devices, shards(): lax.all_to_all(outgoing, 'seq', split_axis=0, concat_axis=0, tiled=True)  7.39 us
    scatter x1, local copies, waits for them, and re-layouts, shards(): page_source = jnp.zeros((total_pages,), jnp.int32).at[page_table].set(jnp...  6.18 us
    all_to_all x1, starting transfers between devices, shards(): lax.all_to_all(outgoing_pages, 'seq', split_axis=0, concat_axis=0, tiled=...  6 us
    dot_general x1, matrix products, attend(): jnp.dot(query_rows, key_part.T, preferred_element_type=jnp.float32)  3.87 us
    reduce_sum x1, other arithmetic, attend(): weight_sum = jnp.sum(weights, axis=1)  2.99 us
  transfers between devices with their start and end apart: 3, of which 2 were waited for; matrix products, arithmetic and copies ran while one was open for 16% of the time, Pallas kernels for 0%

commit v1 on v0

v1 whole, which is shorter than its diff:
```python
import jax
import jax.numpy as jnp
from jax import lax
from jax.sharding import PartitionSpec as P

GROUP = 8
PAGE = 4


ROPE_BASE = 500000.0


def rotate_pos(vector, positions):
    half_dim = vector.shape[-1] // 2
    frequency = ROPE_BASE ** (-(jnp.arange(half_dim, dtype=jnp.float32) * (2.0 / vector.shape[-1])))
    angles = positions.astype(jnp.float32)[..., None] * frequency
    cosine = jnp.cos(angles)
    sine = jnp.sin(angles)
    lower_half = vector[..., :half_dim]
    upper_half = vector[..., half_dim:]
    return jnp.concatenate(
        [lower_half * cosine - upper_half * sine, upper_half * cosine + lower_half * sine], axis=-1
    )


def pick(one_hot, table):
    return jnp.dot(one_hot.astype(jnp.float32), table, precision=lax.Precision.HIGHEST)


def shards(
    pool_kv, pool_slot, passage_order, passage_start, recompute_pos, page_table, fresh_q, fresh_kv
):
    seq_count = lax.axis_size("seq")
    my_index = lax.axis_index("seq")
    page_count = pool_kv.shape[0]
    row_width = pool_kv.shape[1]
    head_dim = fresh_kv.shape[1] // 2
    half_dim = head_dim // 2
    sel_count = fresh_q.shape[0]
    tok_count = page_count * PAGE
    total_pages = seq_count * page_count
    total_toks = seq_count * tok_count
    total_sel = seq_count * sel_count
    bf16 = jnp.bfloat16

    pooled = lax.all_gather(
        pool_kv.reshape(tok_count, 2 * head_dim), "seq", axis=0, tiled=True
    )
    fresh = lax.all_gather(fresh_kv, "seq", axis=0, tiled=True)

    passage_ids = jnp.arange(seq_count, dtype=jnp.int32)
    placed = passage_order[:, None] == passage_ids[None, :]
    slots = jnp.sum(jnp.where(placed, pool_slot[None, :], 0), axis=1)

    frequency = ROPE_BASE ** (-(jnp.arange(half_dim, dtype=jnp.float32) * (2.0 / head_dim)))
    start_angles = passage_start.astype(jnp.float32)[:, None] * frequency
    start_table = jnp.concatenate([jnp.cos(start_angles), jnp.sin(start_angles)], axis=1)
    recompute_rows = recompute_pos.astype(jnp.float32)

    row_ids = jnp.arange(total_pages, dtype=jnp.int32)
    spot = (row_ids % page_count) * seq_count + row_ids // page_count
    row_slot = spot // page_count
    row_page = spot % page_count
    row_hot = row_slot[:, None] == slots[None, :]
    row_passage = jnp.sum(jnp.where(row_hot, passage_ids[None, :], 0), axis=1)
    row_turn = pick(row_hot, start_table)
    row_recompute = pick(row_hot, recompute_rows)
    lane = jnp.arange(PAGE, dtype=jnp.int32)
    row_tok = row_page[:, None] * PAGE + lane[None, :]
    replaced = jnp.any(
        row_recompute[:, None, :] == row_tok[:, :, None].astype(jnp.float32), axis=2
    )
    far = jnp.int32(2**30)
    cached_pos = jnp.where(replaced, far, row_passage[:, None] * tok_count + row_tok).reshape(-1)
    fresh_place = (passage_ids[:, None] * tok_count + recompute_pos).reshape(-1)
    key_pos = jnp.concatenate([cached_pos, fresh_place])

    raw = pooled[:, :head_dim].astype(jnp.float32).reshape(total_pages, PAGE, head_dim)
    cosine = row_turn[:, None, :half_dim]
    sine = row_turn[:, None, half_dim:]
    lower = raw[:, :, :half_dim]
    upper = raw[:, :, half_dim:]
    shifted = jnp.concatenate(
        [lower * cosine - upper * sine, upper * cosine + lower * sine], axis=-1
    ).astype(bf16)
    fresh_pos_all = (passage_start[:, None] + recompute_pos).reshape(-1)
    fresh_keys = rotate_pos(fresh[:, :head_dim].astype(jnp.float32), fresh_pos_all).astype(bf16)
    keys = jnp.concatenate([shifted.reshape(total_toks, head_dim), fresh_keys], axis=0)
    values = jnp.concatenate([pooled[:, head_dim:], fresh[:, head_dim:]], axis=0)

    my_rows = my_index * page_count + jnp.arange(page_count, dtype=jnp.int32)
    source = jnp.sum(
        jnp.where(
            page_table[None, :] == my_rows[:, None],
            jnp.arange(total_pages, dtype=jnp.int32)[None, :],
            0,
        ),
        axis=1,
    )
    source_passage = source // page_count
    source_page = source % page_count
    source_hot = source_passage[:, None] == passage_ids[None, :]
    source_spot = (
        jnp.sum(jnp.where(source_hot, slots[None, :], 0), axis=1) * page_count + source_page
    )
    source_row = (source_spot % seq_count) * page_count + source_spot // seq_count
    source_recompute = pick(source_hot, recompute_rows)
    source_tok = source_page[:, None] * PAGE + lane[None, :]
    match = source_recompute[:, None, :] == source_tok[:, :, None].astype(jnp.float32)
    sel_ids = jnp.arange(sel_count, dtype=jnp.int32)
    sel_at = jnp.sum(jnp.where(match, sel_ids[None, None, :] + 1, 0), axis=2)
    token_at = jnp.where(
        sel_at > 0,
        total_toks + source_passage[:, None] * sel_count + sel_at - 1,
        source_row[:, None] * PAGE + lane[None, :],
    ).reshape(-1)
    choose = (
        token_at[:, None] == jnp.arange(total_toks + total_sel, dtype=jnp.int32)[None, :]
    ).astype(bf16)
    page_keys = jnp.dot(choose, keys, preferred_element_type=jnp.float32).astype(bf16)
    page_values = jnp.dot(choose, values, preferred_element_type=jnp.float32).astype(bf16)
    decode_cache = jnp.concatenate([page_keys, page_values], axis=1).reshape(
        page_count, row_width
    )

    mine = (passage_ids == my_index)[:, None]
    picked = jnp.sum(jnp.where(mine, recompute_pos, 0), axis=0)
    start_pos = jnp.sum(jnp.where(mine[:, 0], passage_start, 0))
    queries = rotate_pos(
        fresh_q.reshape(sel_count, GROUP, head_dim).astype(jnp.float32),
        (start_pos + picked)[:, None],
    ).astype(bf16)
    query_rows = queries.reshape(-1, head_dim)
    query_pos = jnp.repeat(my_index * tok_count + picked, GROUP)
    attended = attend(query_rows, query_pos, keys, values, key_pos)
    return (attended.reshape(sel_count, GROUP * head_dim), decode_cache)


def attend(query_rows, query_pos, keys, values, key_pos):
    score_scale = keys.shape[1] ** (-0.5)
    scores = jnp.dot(query_rows, keys.T, preferred_element_type=jnp.float32) * score_scale
    allowed = key_pos[None, :] <= query_pos[:, None]
    peak = jnp.max(jnp.where(allowed, scores, -jnp.inf), axis=1)
    weights = jnp.where(allowed, jnp.exp(scores - peak[:, None]), 0.0)
    weight_sum = jnp.sum(weights, axis=1)
    weighted = jnp.dot(weights.astype(jnp.bfloat16), values, preferred_element_type=jnp.float32)
    return (weighted / weight_sum[:, None]).astype(jnp.bfloat16)


def solution(mesh):
    placed = (
        P(("groups", "seq"), None),
        P("groups"),
        P("groups"),
        P("groups"),
        P("groups", None),
        P("groups"),
        P(("groups", "seq"), None),
        P(("groups", "seq"), None),
    )
    return jax.shard_map(
        shards,
        mesh=mesh,
        in_specs=placed,
        out_specs=(P(("groups", "seq"), None), P(("groups", "seq"), None)),
        check_vma=False,
    )
```

time: 125 us -> 88.9 us (0.71)
  blocking collectives: 0 us -> 24.9 us
  other arithmetic: 31.6 us -> 12.1 us
  waiting for transfers between devices: 31.8 us -> 16 us
  local copies, waits for them, and re-layouts: 23.2 us -> 7.72 us
  starting transfers between devices: 13.4 us -> 0.04 us
  matrix products: 6.5 us -> 13.5 us
  between operations: 17.5 us -> 14.4 us
    all_gather x0 -> x1, blocking collectives: none -> 24.9 us  [shards(): fresh = lax.all_gather(fresh_kv, 'seq', axis=0, tiled=True)]
    select_n x9 -> x3, other arithmetic: 23.7 us -> 0.04 us  [the longest x1 0.02 us: shards(): row_slot = spot // page_count]
    all_to_all x2 -> x0, starting transfers between devices: 13.4 us -> none  [the longest x1 7.39 us: shards(): lax.all_to_all(outgoing, 'seq', split_axis=0, concat_axis=0, tiled=True)]
    scatter x6 -> x0, local copies, waits for them, and re-layouts: 10.9 us -> none  [the longest x1 6.18 us: shards(): page_source = jnp.zeros((total_pages,), jnp.int32).at[page_table].set(jnp...]
    all_to_all x2 -> x0, waiting for transfers between devices: 10.1 us -> none  [the longest x1 10.1 us: shards(): lax.all_to_all(outgoing_pages, 'seq', split_axis=0, concat_axis=0, tiled=...]
    dot_general x2 -> x7, matrix products: 6.5 us -> 13.5 us  [the longest x1 3.23 us: attend(): jnp.dot(query_rows, keys.T, preferred_element_type=jnp.float32)]
    all_gather x1, waiting for transfers between devices: 21.7 us -> 16 us  [shards(): lax.all_gather(pool_kv.reshape(tok_count, 2 * head_dim), 'seq', axis=0, t...]
    gather x5 -> x0, local copies, waits for them, and re-layouts: 4.3 us -> none  [the longest x1 1.46 us: shards(): decode_cache = landed[source_dev * capacity + rank_in]]
  transfers between devices with their start and end apart: 3 -> 1, of which waited for: 2 -> 1; matrix products, arithmetic and copies ran while one was open for 16% -> 11% of each run, Pallas kernels for 0% -> 0%
where the time goes in v1:
time: 88.9 us; the launch traced here: 88.6 us
  blocking collectives  24.9 us (28%)
  waiting for transfers between devices  16 us (18%)
  between operations  14.4 us (16%)
  matrix products  13.5 us (15%)
  other arithmetic  12.1 us (14%)
  local copies, waits for them, and re-layouts  7.72 us (9%)
    all_gather x1, blocking collectives, shards(): fresh = lax.all_gather(fresh_kv, 'seq', axis=0, tiled=True)  24.9 us
    all_gather x1, waiting for transfers between devices, shards(): lax.all_gather(pool_kv.reshape(tok_count, 2 * head_dim), 'seq', axis=0, t...  16 us
    another operation x2, other arithmetic  3.53 us
    dot_general x1, matrix products, attend(): jnp.dot(query_rows, keys.T, preferred_element_type=jnp.float32)  3.23 us
    reduce_sum x1, other arithmetic, attend(): weight_sum = jnp.sum(weights, axis=1)  3.11 us
    dot_general x1, matrix products, shards(): jnp.dot(choose, keys, preferred_element_type=jnp.float32).astype(bf16)  3.1 us
    dot_general x1, matrix products, attend(): jnp.dot(weights.astype(jnp.bfloat16), values, preferred_element_type=jnp....  2.84 us
    dot_general x1, matrix products, shards(): jnp.dot(choose, values, preferred_element_type=jnp.float32).astype(bf16)  2.54 us
  transfers between devices with their start and end apart: 1, of which 1 were waited for; matrix products, arithmetic and copies ran while one was open for 11% of the time, Pallas kernels for 0%

profile of v1, /device:TPU:0, one launch (start us, length us, event | category | flops | bytes accessed | tf_op | source)
XLA Modules:
  0.0 88.6 jit_solution(6982607448881617430)
XLA Ops:
  7.2 1.7 %reshape.340 = bf16[384,256]{1,0:T(8,128)(2,1)} reshape(bf16[96,1024]{1,0:T(8,128)(2,1)} %param.8) | data formatting | bytes 393216 | tf_op jit(solution)/shard_map/reshape | solution.py:47
  9.0 0.9 select_reduce_fusion.4
  10.0 1.0 %fusion.27 = f32[1536,56]{0,1:T(8,128)S(1)} fusion(s32[1536]{0:T(1024)S(1)} %add_select_fusion.2, s32[16]{0:T(128)S(1)} %select_reduce_fusion.4, s32[16,56]{1,0:T(8,128)} %param.12), kind=kOutput, calls=%fused_computation.39 | convolution fusion | flops 16540544 | bytes 353856 | tf_op jit(solution)/shard_map/dot_general | solution.py:27
  11.0 0.8 broadcast_add_fusion
  12.0 0.2 compare_reduce_fusion
  12.2 0.3 copy.32
  12.5 0.4 select_n.152
  12.9 1.4 %fusion.71 = (f32[16]{0:T(128)S(1)}, s32[]{:T(128)}) fusion(s32[16]{0:T(128)} %param.11, s32[]{:T(128)S(6)} %axis_index.12), kind=kLoop, calls=%fused_computation.126 | loop fusion | flops 63 | bytes 136 | tf_op jit(solution)/shard_map/convert_element_type | solution.py:56
  14.3 0.6 broadcast_add_fusion.1
  15.1 24.9 %all_gather.7 = bf16[896,256]{1,0:T(8,128)(2,1)S(1)} all-gather(bf16[56,256]{1,0:T(8,128)(2,1)S(1)} %copy-done.2), channel_id=1, replica_groups=mesh['groups'=2,'seq'=16] {'seq'}, dimensions={0}, use_global_device_ids=true | all-gather | bytes 487424 | tf_op jit(solution)/shard_map/all_gather | solution.py:49
  40.0 0.2 copy.39
  40.3 0.9 %fusion.22 = (bf16[896,64]{0,1:T(8,128)(2,1)S(1)}, bf16[896,64]{0,1:T(8,128)(2,1)S(1)}) fusion(f32[896,128]{0,1:T(8,128)S(1)} %convert_element_type.78, f32[64]{0:T(128)S(1)} %negate_power_fusion, f32[896]{0:T(1024)S(1)} %convert_element_type.80), kind=kLoop, calls=%fused_computation.28 | loop fusion | flops 516096 | bytes 691968 | tf_op jit(solution)/shard_map/convert.2
  41.3 0.2 copy.36
  41.6 0.6 fusion.25
  42.3 0.3 copy.34
  42.5 0.3 copy.33
  42.9 0.2 select_reduce_fusion
  43.3 0.2 fusion.54
  43.9 0.2 multiply_cosine_fusion.1
  44.1 0.1 fusion.29
  44.2 16.0 %all-gather.2.cloned.1.call-done = bf16[6144,256]{1,0:T(8,128)(2,1)} async-done(((bf16[384,256]{1,0:T(8,128)(2,1)}), bf16[6144,256]{1,0:T(8,128)(2,1)}) %all-gather.2.cloned.1.call-update) | async-done | bytes 3145744 | tf_op jit(solution)/shard_map/all_gather | solution.py:46
  60.2 2.1 %fusion.68 = (bf16[6144,128]{1,0:T(8,128)(2,1)S(1)}, bf16[6144,128]{1,0:T(8,128)(2,1)S(1)}) fusion(bf16[6144,256]{1,0:T(8,128)(2,1)} %all-gather.2.cloned.1.call-done), kind=kLoop, calls=%fused_computation.123 | loop fusion | bytes 6291456 | tf_op jit(solution)/shard_map/slice | solution.py:78
  62.3 0.4 convert.30
  62.6 2.6 %subtract_convert_fusion = (bf16[1536,4,64]{2,1,0:T(4,128)(2,1)S(1)}, bf16[1536,4,64]{2,1,0:T(4,128)(2,1)S(1)}) fusion(f32[1536,4,128]{2,1,0:T(4,128)S(1)} %convert.30, f32[1536,64]{1,0:T(8,128)S(1)} %copy.34, f32[1536,64]{1,0:T(8,128)S(1)} %copy.33), kind=kLoop, calls=%fused_computation.12 | loop fusion | flops 3145728 | bytes 5505024 | tf_op jit(solution)/shard_map/convert.7
  65.3 3.1 %fusion.9 = bf16[384,128]{0,1:T(8,128)(2,1)S(1)} fusion(s32[384]{0:T(512)S(1)} %select_n.165, bf16[896,128]{1,0:T(8,128)(2,1)S(1)} %copy.36, bf16[6144,64]{1,0:T(8,128)(2,1)S(1)} %bitcast.15, bf16[6144,64]{1,0:T(8,128)(2,1)S(1)} %bitcast.13), kind=kOutput, calls=%fused_computation.16 | convolution fusion | flops 700219392 | bytes 1902080 | tf_op jit(solution)/shard_map/dot_general | solution.py:120
  68.4 3.2 %fusion = (f32[448]{0:T(512)S(1)}, f32[448,7040]{1,0:T(8,128)S(1)}) fusion(s32[7040]{0:T(1024)S(1)} %pad_add_fusion, s32[448]{0:T(512)S(1)} %le.16, bf16[896,128]{1,0:T(8,128)(2,1)S(1)} %copy.36, bf16[6144,64]{1,0:T(8,128)(2,1)S(1)} %bitcast.16, bf16[6144,64]{1,0:T(8,128)(2,1)S(1)} %bitcast.14, bf16[448,64]{1,0:T(8,128)(2,1)S(1)} %get-tuple-element.15, ...), kind=kOutput, calls=%fused_computation.2 | convolution fusion | flops 825654848 | bytes 14564352 | tf_op jit(solution)/shard_map/dot_general | solution.py:141
  71.6 3.1 %fusion.3 = f32[448]{0:T(512)S(1)} fusion(f32[448,7040]{1,0:T(8,128)S(1)} %get-tuple-element.30, f32[448]{0:T(512)S(1)} %get-tuple-element.29, s32[7040]{0:T(1024)S(1)} %pad_add_fusion, s32[448]{0:T(512)S(1)} %le.16), kind=kLoop, calls=%fused_computation.6 | loop fusion | flops 15769152 | bytes 12649216 | tf_op jit(solution)/shard_map/reduce_sum | solution.py:145
  74.7 2.5 %fusion.10 = bf16[384,128]{0,1:T(8,128)(2,1)S(1)} fusion(bf16[896,128]{1,0:T(8,128)(2,1)S(1)} %get-tuple-element.13, bf16[6144,128]{1,0:T(8,128)(2,1)S(1)} %get-tuple-element.7, s32[384]{0:T(512)S(1)} %select_n.165), kind=kOutput, calls=%fused_computation.17 | convolution fusion | flops 698417152 | bytes 1902080 | tf_op jit(solution)/shard_map/dot_general | solution.py:121
  77.2 2.8 %fusion.14 = bf16[448,128]{1,0:T(8,128)(2,1)S(1)} fusion(bf16[896,128]{1,0:T(8,128)(2,1)S(1)} %get-tuple-element.13, bf16[6144,128]{1,0:T(8,128)(2,1)S(1)} %get-tuple-element.7, f32[448,7040]{1,0:T(8,128)S(1)} %get-tuple-element.30, f32[448]{0:T(512)S(1)} %get-tuple-element.29, s32[7040]{0:T(1024)S(1)} %pad_add_fusion, s32[448]{0:T(512)S(1)} %le.16, ...), kind=kOutput, calls=%fused_computation.19 | convolution fusion | flops 826892288 | bytes 14566144 | tf_op jit(solution)/shard_map/dot_general | solution.py:146
  80.1 0.7 reshape.343
  80.8 0.1 copy.38
  81.0 0.8 reshape.344
  (41 shorter events, 1.4 us)
Async XLA Ops:
  7.2 7.9 %copy-start.2 = (bf16[56,256]{1,0:T(8,128)(2,1)S(1)}, bf16[56,256]{1,0:T(8,128)(2,1)}, u32[]{:S(2)}) copy-start(bf16[56,256]{1,0:T(8,128)(2,1)} %param.15) | copy-start | bytes 86020
  7.2 53.0 %all-gather.2.cloned.1.call-start = ((), (), s32[]{:S(2)}) async-start(), calls=%async_computation | async-start | bytes 3342336 | tf_op jit(solution)/shard_map/all_gather | solution.py:46
  40.3 2.5 %copy-start = (bf16[56,1024]{1,0:T(8,128)(2,1)S(1)}, bf16[56,1024]{1,0:T(8,128)(2,1)}, u32[]{:S(2)}) copy-start(bf16[56,1024]{1,0:T(8,128)(2,1)} %param.14) | copy-start | bytes 344068
  41.3 1.7 %copy-start.3 = (s32[1536]{0:T(1024)S(1)}, s32[1536]{0:T(1024)}, u32[]{:S(2)}) copy-start(s32[1536]{0:T(1024)} %param.13) | copy-start | bytes 18436
  41.3 2.0 %copy-start.1 = (s32[16,56]{1,0:T(8,128)S(1)}, s32[16,56]{1,0:T(8,128)}, u32[]{:S(2)}) copy-start(s32[16,56]{1,0:T(8,128)} %param.12) | copy-start | bytes 10756
Sparse Core Ops, SparseCore 0:
  10.8 49.2 all-gather.1

commit v2 on v1

--- a/solution.py
+++ b/solution.py
@@ -1,6 +1,8 @@
 import jax
 import jax.numpy as jnp
 from jax import lax
+from jax.experimental import pallas as pl
+from jax.experimental.pallas import tpu as pltpu
 from jax.sharding import PartitionSpec as P
 
 GROUP = 8
@@ -21,6 +23,155 @@
     return jnp.concatenate(
         [lower_half * cosine - upper_half * sine, upper_half * cosine + lower_half * sine], axis=-1
     )
+
+
+MESH = pl.DeviceIdType.MESH
+
+
+def spread_kernel(count, block_ref, all_ref, send_sem, recv_sem, own_sem):
+    rows = block_ref.shape[0]
+    cut = rows * 3 // 5 // 16 * 16
+    parts = (pl.ds(0, cut), pl.ds(cut, rows - cut))
+    length = count // 4
+    me = lax.axis_index("seq")
+    at = me // 4
+    inner = lax.rem(me, 4)
+    core = lax.rem(inner, 2)
+    across_inner = lax.rem(inner + 2, 4)
+    across = at * 4 + across_inner
+    sibling = me + 1 - 2 * core
+    twin_inner = inner + 1 - 2 * core
+    up, down = me + 4, me - 4
+    has_up, has_down = at < length - 1, at > 0
+
+    barrier = pltpu.get_barrier_semaphore()
+
+    def greet(device):
+        pl.semaphore_signal(barrier, inc=1, device_id={"seq": device}, device_id_type=MESH)
+
+    greet(across)
+    greet(sibling)
+    pl.when(has_up)(lambda: greet(up))
+    pl.when(has_down)(lambda: greet(down))
+    pl.semaphore_wait(barrier, 2 + jnp.where(has_up, 1, 0) + jnp.where(has_down, 1, 0))
+
+    def copy(part, block, way, device, own=False):
+        source = block_ref.at[parts[part]] if own else all_ref.at[block, parts[part]]
+        return pltpu.make_async_remote_copy(
+            src_ref=source,
+            dst_ref=all_ref.at[block, parts[part]],
+            send_sem=send_sem.at[way, part, block],
+            recv_sem=recv_sem.at[part, block],
+            device_id={"seq": device},
+            device_id_type=MESH,
+        )
+
+    def begin(part, block, way, device, own=False):
+        copy(part, block, way, device, own).start()
+
+    def arrive(part, block):
+        copy(part, block, 0, sibling).wait_recv()
+
+    local = pltpu.make_async_copy(block_ref, all_ref.at[me], own_sem)
+    local.start()
+
+    def send_own(act):
+        act(1, me, 2, across, True)
+        pl.when(has_up)(lambda: act(0, me, 0, up, True))
+        pl.when(has_down)(lambda: act(0, me, 1, down, True))
+        pl.when(has_up)(lambda: act(1, me, 0, up, True))
+        pl.when(has_down)(lambda: act(1, me, 1, down, True))
+        act(0, me, 2, across, True)
+        act(1, me, 3, sibling, True)
+        act(0, me, 3, sibling, True)
+
+    def pass_across_first(act):
+        pl.when(has_up)(lambda: act(1, across, 0, up))
+        pl.when(has_down)(lambda: act(1, across, 1, down))
+        act(1, across, 3, sibling)
+
+    def each(step, act, wait):
+        for way, exists, more, device, place in (
+            (0, at - step >= 0, has_up, up, at - step),
+            (1, at + step < length, has_down, down, at + step),
+        ):
+            for part, where, cross in ((0, inner, True), (1, inner, False), (1, across_inner, False)):
+                block = place * 4 + where
+
+                @pl.when(exists)
+                def _(part=part, block=block, cross=cross, way=way, more=more, device=device):
+                    if wait:
+                        arrive(part, block)
+                    pl.when(more)(lambda: act(part, block, way, device))
+                    if cross:
+                        act(part, block, 2, across)
+                    act(part, block, 3, sibling)
+
+    def crossed(step, act, wait):
+        for exists, place in ((at - step >= 0, at - step), (at + step < length, at + step)):
+
+            @pl.when(exists)
+            def _(place=place):
+                block = place * 4 + across_inner
+                if wait:
+                    arrive(0, block)
+                act(0, block, 3, sibling)
+
+    def crossed_here(act, wait):
+        if wait:
+            arrive(0, across)
+        act(0, across, 3, sibling)
+
+    send_own(begin)
+    arrive(1, across)
+    pass_across_first(begin)
+
+    @pl.loop(1, length)
+    def _(step):
+        each(step, begin, True)
+
+    crossed_here(begin, True)
+
+    @pl.loop(1, length)
+    def _(step):
+        crossed(step, begin, True)
+
+    @pl.loop(0, length)
+    def _(place):
+        for other in range(2):
+            block = place * 4 + other * 2 + lax.rem(core + 1, 2)
+            arrive(0, block)
+            arrive(1, block)
+
+    def settle(part, block, way, device, own=False):
+        copy(part, block, way, device, own).wait_send()
+
+    send_own(settle)
+    pass_across_first(settle)
+
+    @pl.loop(1, length)
+    def _(step):
+        each(step, settle, False)
+        crossed(step, settle, False)
+
+    crossed_here(settle, False)
+    local.wait()
+
+
+def spread(block, count):
+    rows, width = block.shape
+    return pl.pallas_call(
+        lambda *refs: spread_kernel(count, *refs),
+        out_shape=jax.ShapeDtypeStruct((count, rows, width), block.dtype),
+        in_specs=[pl.BlockSpec(memory_space=pltpu.VMEM)],
+        out_specs=pl.BlockSpec(memory_space=pl.ANY),
+        scratch_shapes=[
+            pltpu.SemaphoreType.DMA((4, 2, count)),
+            pltpu.SemaphoreType.DMA((2, count)),
+            pltpu.SemaphoreType.DMA,
+        ],
+        compiler_params=pltpu.CompilerParams(collective_id=0, has_side_effects=True),
+    )(block)
 
 
 def pick(one_hot, table):
@@ -39,14 +190,11 @@
     sel_count = fresh_q.shape[0]
     tok_count = page_count * PAGE
     total_pages = seq_count * page_count
-    total_toks = seq_count * tok_count
-    total_sel = seq_count * sel_count
     bf16 = jnp.bfloat16
 
-    pooled = lax.all_gather(
-        pool_kv.reshape(tok_count, 2 * head_dim), "seq", axis=0, tiled=True
-    )
-    fresh = lax.all_gather(fresh_kv, "seq", axis=0, tiled=True)
+    unit = tok_count + sel_count
+    block = jnp.concatenate([pool_kv.reshape(tok_count, 2 * head_dim), fresh_kv], axis=0)
+    everything = spread(block, seq_count)
 
     passage_ids = jnp.arange(seq_count, dtype=jnp.int32)
     placed = passage_order[:, None] == passage_ids[None, :]
@@ -72,21 +220,30 @@
     )
     far = jnp.int32(2**30)
     cached_pos = jnp.where(replaced, far, row_passage[:, None] * tok_count + row_tok).reshape(-1)
-    fresh_place = (passage_ids[:, None] * tok_count + recompute_pos).reshape(-1)
-    key_pos = jnp.concatenate([cached_pos, fresh_place])
-
-    raw = pooled[:, :head_dim].astype(jnp.float32).reshape(total_pages, PAGE, head_dim)
-    cosine = row_turn[:, None, :half_dim]
-    sine = row_turn[:, None, half_dim:]
+    fresh_place = passage_ids[:, None] * tok_count + recompute_pos
+    key_pos = jnp.concatenate([cached_pos.reshape(seq_count, tok_count), fresh_place], axis=1)
+    key_pos = key_pos.reshape(-1)
+
+    fresh_angles = (passage_start[:, None] + recompute_pos).astype(jnp.float32)[
+        :, :, None
+    ] * frequency
+    fresh_turn = jnp.concatenate([jnp.cos(fresh_angles), jnp.sin(fresh_angles)], axis=-1)
+    cached_turn = jnp.broadcast_to(
+        row_turn.reshape(seq_count, page_count, 1, head_dim),
+        (seq_count, page_count, PAGE, head_dim),
+    ).reshape(seq_count, tok_count, head_dim)
+    turn = jnp.concatenate([cached_turn, fresh_turn], axis=1)
+    raw = everything[:, :, :head_dim].astype(jnp.float32)
+    cosine = turn[:, :, :half_dim]
+    sine = turn[:, :, half_dim:]
     lower = raw[:, :, :half_dim]
     upper = raw[:, :, half_dim:]
-    shifted = jnp.concatenate(
-        [lower * cosine - upper * sine, upper * cosine + lower * sine], axis=-1
-    ).astype(bf16)
-    fresh_pos_all = (passage_start[:, None] + recompute_pos).reshape(-1)
-    fresh_keys = rotate_pos(fresh[:, :head_dim].astype(jnp.float32), fresh_pos_all).astype(bf16)
-    keys = jnp.concatenate([shifted.reshape(total_toks, head_dim), fresh_keys], axis=0)
-    values = jnp.concatenate([pooled[:, head_dim:], fresh[:, head_dim:]], axis=0)
+    keys = (
+        jnp.concatenate([lower * cosine - upper * sine, upper * cosine + lower * sine], axis=-1)
+        .astype(bf16)
+        .reshape(seq_count * unit, head_dim)
+    )
+    values = everything[:, :, head_dim:].reshape(seq_count * unit, head_dim)
 
     my_rows = my_index * page_count + jnp.arange(page_count, dtype=jnp.int32)
     source = jnp.sum(
@@ -103,7 +260,7 @@
     source_spot = (
         jnp.sum(jnp.where(source_hot, slots[None, :], 0), axis=1) * page_count + source_page
     )
-    source_row = (source_spot % seq_count) * page_count + source_spot // seq_count
+    source_row = (source_spot % seq_count) * unit + source_spot // seq_count * PAGE
     source_recompute = pick(source_hot, recompute_rows)
     source_tok = source_page[:, None] * PAGE + lane[None, :]
     match = source_recompute[:, None, :] == source_tok[:, :, None].astype(jnp.float32)
@@ -111,11 +268,11 @@
     sel_at = jnp.sum(jnp.where(match, sel_ids[None, None, :] + 1, 0), axis=2)
     token_at = jnp.where(
         sel_at > 0,
-        total_toks + source_passage[:, None] * sel_count + sel_at - 1,
-        source_row[:, None] * PAGE + lane[None, :],
+        source_passage[:, None] * unit + tok_count + sel_at - 1,
+        source_row[:, None] + lane[None, :],
     ).reshape(-1)
     choose = (
-        token_at[:, None] == jnp.arange(total_toks + total_sel, dtype=jnp.int32)[None, :]
+        token_at[:, None] == jnp.arange(seq_count * unit, dtype=jnp.int32)[None, :]
     ).astype(bf16)
     page_keys = jnp.dot(choose, keys, preferred_element_type=jnp.float32).astype(bf16)
     page_values = jnp.dot(choose, values, preferred_element_type=jnp.float32).astype(bf16)

time: 88.9 us -> 74 us (0.83)
  Pallas kernels: 0 us -> 32.4 us
  blocking collectives: 24.9 us -> 0 us
  waiting for transfers between devices: 16 us -> 0 us
  between operations: 14.4 us -> 1.03 us
  other arithmetic: 12.1 us -> 16.6 us
  matrix products: 13.5 us -> 16.3 us
    pallas_call x0 -> x1, Pallas kernels: none -> 32.4 us  [spread(): pl.pallas_call(lambda *refs: spread_kernel(count, *refs), out_shape=jax.S...]
    all_gather x1 -> x0, blocking collectives: 24.9 us -> none  [shards(): fresh = lax.all_gather(fresh_kv, 'seq', axis=0, tiled=True)]
    all_gather x1 -> x0, waiting for transfers between devices: 16 us -> none  [shards(): lax.all_gather(pool_kv.reshape(tok_count, 2 * head_dim), 'seq', axis=0, t...]
    convert_element_type x2 -> x1, other arithmetic: 1.4 us -> 4.84 us  [shards(): raw = everything[:, :, :head_dim].astype(jnp.float32)]
    slice x5 -> x0, local copies, waits for them, and re-layouts: 2.7 us -> none  [the longest x1 2.08 us: shards(): pooled[:, :head_dim].astype(jnp.float32)]
    dot_general x1, matrix products: 2.54 us -> 4.37 us  [shards(): jnp.dot(choose, values, preferred_element_type=jnp.float32).astype(bf16)]
    concatenate x1 -> x3, other arithmetic: 0.01 us -> 1.8 us  [the longest x1 1.45 us: shards(): jnp.concatenate([pool_kv.reshape(tok_count, 2 * head_dim), fresh_kv], axi...]
    cos x0 -> x1, other arithmetic: none -> 1.66 us  [shards(): jnp.cos(fresh_angles)]
  transfers between devices with their start and end apart: 1 -> 0, of which waited for: 1 -> 0; matrix products, arithmetic and copies ran while one was open for 11% -> 0% of each run, Pallas kernels for 0% -> 0%
where the time goes in v2:
time: 74 us; the launch traced here: 73.7 us
  Pallas kernels  32.4 us (44%)
  other arithmetic  16.6 us (22%)
  matrix products  16.3 us (22%)
  local copies, waits for them, and re-layouts  7.36 us (10%)
  between operations  1.03 us (1%)
    pallas_call x1, Pallas kernels, spread(): pl.pallas_call(lambda *refs: spread_kernel(count, *refs), out_shape=jax.S...  32.4 us
    convert_element_type x1, other arithmetic, shards(): raw = everything[:, :, :head_dim].astype(jnp.float32)  4.84 us
    dot_general x1, matrix products, shards(): jnp.dot(choose, values, preferred_element_type=jnp.float32).astype(bf16)  4.37 us
    dot_general x1, matrix products, attend(): jnp.dot(weights.astype(jnp.bfloat16), values, preferred_element_type=jnp....  4.09 us
    dot_general x1, matrix products, attend(): jnp.dot(query_rows, keys.T, preferred_element_type=jnp.float32)  3.29 us
    dot_general x1, matrix products, shards(): jnp.dot(choose, keys, preferred_element_type=jnp.float32).astype(bf16)  3.17 us
    reduce_sum x1, other arithmetic, attend(): weight_sum = jnp.sum(weights, axis=1)  3.1 us
    another operation x1, other arithmetic  2.19 us

profile of v2, /device:TPU:0, one launch (start us, length us, event | category | flops | bytes accessed | tf_op | source)
XLA Modules:
  0.0 73.7 jit_solution(12496336347889492806)
XLA Ops:
  0.6 1.1 %reshape.322 = bf16[384,256]{1,0:T(8,128)(2,1)S(1)} reshape(bf16[96,1024]{1,0:T(8,128)(2,1)} %param.8) | data formatting | bytes 393216 | tf_op jit(solution)/shard_map/reshape | solution.py:196
  1.7 1.4 %pad_maximum_fusion.3.refs_0_ = bf16[440,256]{1,0:T(8,128)(2,1)} fusion(bf16[56,256]{1,0:T(8,128)(2,1)} %param.15, bf16[384,256]{1,0:T(8,128)(2,1)S(1)} %reshape.322), kind=kLoop, calls=%fused_computation.28 | loop fusion | flops 450560 | bytes 450560 | tf_op jit(solution)/shard_map/concatenate | solution.py:196
  3.1 32.4 %shard_map.95 = bf16[16,440,256]{2,1,0:T(8,128)(2,1)} custom-call(bf16[440,256]{1,0:T(8,128)(2,1)} %pad_maximum_fusion.3.refs_0_), custom_call_target="tpu_custom_call" | custom-call | tf_op jit(solution)/shard_map/pallas_call | solution.py:163
  35.6 4.8 %slice_convert_fusion = (f32[16,440,128]{2,1,0:T(8,128)}, bf16[16,440,128]{2,1,0:T(8,128)(2,1)}) fusion(bf16[16,440,256]{2,1,0:T(8,128)(2,1)} %shard_map.95), kind=kLoop, calls=%fused_computation.15 | loop fusion | flops 901120 | bytes 9011200 | tf_op jit(solution)/shard_map/convert_element_type | solution.py:236
  40.6 0.2 select_reduce_fusion.4
  40.8 0.3 fusion.20
  41.2 0.2 compare_reduce_fusion
  41.4 0.4 copy.23
  41.8 0.5 reduce_or.12
  43.0 0.1 add.292
  43.2 0.6 select_reduce_fusion.5
  43.9 0.6 broadcast_add_fusion.1
  44.7 1.7 %multiply_cosine_fusion = (f32[16,56,64]{2,1,0:T(8,128)S(1)}, f32[16,56,64]{2,1,0:T(8,128)S(1)}) fusion(f32[64]{0:T(128)S(1)} %negate_power_fusion, f32[16,56]{1,0:T(8,128)S(1)} %get-tuple-element.13), kind=kLoop, calls=%fused_computation.22 | loop fusion | flops 57344 | bytes 462592 | tf_op jit(solution)/shard_map/cos | solution.py:230
  46.4 0.1 multiply_cosine_fusion.2
  46.5 0.9 %fusion.18 = f32[1536,128]{1,0:T(8,128)S(1)} fusion(s32[1536]{0:T(1024)S(1)} %add_select_fusion.5, s32[16]{0:T(128)S(1)} %select_reduce_fusion.4, f32[16,64]{1,0:T(8,128)S(1)} %get-tuple-element.18, f32[16,64]{1,0:T(8,128)S(1)} %get-tuple-element.17), kind=kOutput, calls=%fused_computation.30 | convolution fusion | flops 37775360 | bytes 800832 | tf_op jit(solution)/shard_map/dot_general | solution.py:178
  47.4 0.5 broadcast_in_dim.145
  47.9 0.3 maximum_maximum_fusion
  48.3 1.7 %copy-done = f32[16,440,128]{2,1,0:T(8,128)S(1)} copy-done((f32[16,440,128]{2,1,0:T(8,128)S(1)}, f32[16,440,128]{2,1,0:T(8,128)}, u32[]{:S(2)}) %copy-start) | copy-done | bytes 3604504
  49.9 2.2 %subtract_convert_fusion = (bf16[16,440,64]{2,1,0:T(8,128)(2,1)S(1)}, bf16[16,440,64]{2,1,0:T(8,128)(2,1)S(1)}) fusion(f32[16,440,128]{2,1,0:T(8,128)S(1)} %maximum_maximum_fusion, f32[16,440,128]{2,1,0:T(8,128)S(1)} %copy-done), kind=kLoop, calls=%fused_computation.13 | loop fusion | flops 3604480 | bytes 9011200 | tf_op jit(solution)/shard_map/convert.4
  52.2 0.2 multiply_cosine_fusion.1
  52.4 0.1 fusion.22
  52.6 3.3 %fusion = (f32[448]{0:T(512)S(1)}, f32[448,7040]{1,0:T(8,128)S(1)}) fusion(s32[7040]{0:T(1024)S(1)} %le.17, s32[448]{0:T(512)S(1)} %le.19, bf16[7040,64]{1,0:T(8,128)(2,1)S(1)} %bitcast.21, bf16[7040,64]{1,0:T(8,128)(2,1)S(1)} %bitcast.19, bf16[448,64]{1,0:T(8,128)(2,1)S(1)} %get-tuple-element.9, bf16[448,64]{1,0:T(8,128)(2,1)S(1)} %get-tuple-element.8), kind=kOutput, calls=%fused_computation.2 | convolution fusion | flops 823852608 | bytes 14564352 | tf_op jit(solution)/shard_map/dot_general | solution.py:298
  55.9 3.1 %fusion.3 = f32[448]{0:T(512)S(1)} fusion(f32[448,7040]{1,0:T(8,128)S(1)} %get-tuple-element.26, f32[448]{0:T(512)S(1)} %get-tuple-element.25, s32[7040]{0:T(1024)S(1)} %le.17, s32[448]{0:T(512)S(1)} %le.19), kind=kLoop, calls=%fused_computation.6 | loop fusion | flops 15769152 | bytes 12649216 | tf_op jit(solution)/shard_map/reduce_sum | solution.py:302
  59.0 4.1 %fusion.14 = bf16[448,128]{1,0:T(8,128)(2,1)S(1)} fusion(bf16[7040,128]{1,0:T(8,128)(2,1)} %bitcast.23, f32[448,7040]{1,0:T(8,128)S(1)} %get-tuple-element.26, f32[448]{0:T(512)S(1)} %get-tuple-element.25, s32[7040]{0:T(1024)S(1)} %le.17, s32[448]{0:T(512)S(1)} %le.19, f32[448]{0:T(512)S(1)} %fusion.3), kind=kOutput, calls=%fused_computation.20 | convolution fusion | flops 823287808 | bytes 14566144 | tf_op jit(solution)/shard_map/dot_general | solution.py:303
  63.1 0.7 reshape.325
  63.8 0.2 select_reduce_fusion
  64.1 0.2 fusion.54
  64.5 0.1 copy.27
  65.2 4.4 %fusion.10 = bf16[384,128]{0,1:T(8,128)(2,1)S(1)} fusion(bf16[7040,128]{1,0:T(8,128)(2,1)} %bitcast.24, s32[384]{0:T(512)S(1)} %add_select_fusion.7), kind=kOutput, calls=%fused_computation.18 | convolution fusion | flops 694812672 | bytes 1902080 | tf_op jit(solution)/shard_map/dot_general | solution.py:278
  69.6 3.2 %fusion.9 = bf16[384,128]{0,1:T(8,128)(2,1)S(1)} fusion(s32[384]{0:T(512)S(1)} %add_select_fusion.7, bf16[7040,64]{1,0:T(8,128)(2,1)S(1)} %bitcast.22, bf16[7040,64]{1,0:T(8,128)(2,1)S(1)} %bitcast.20), kind=kOutput, calls=%fused_computation.17 | convolution fusion | flops 698417152 | bytes 1902080 | tf_op jit(solution)/shard_map/dot_general | solution.py:277
  72.8 0.1 copy.29
  72.9 0.8 %reshape.326 = bf16[96,1024]{1,0:T(8,128)(2,1)} reshape(bf16[384,256]{1,0:T(8,128)(2,1)S(1)} %copy.29) | data formatting | bytes 393216 | tf_op jit(solution)/shard_map/reshape | solution.py:279
  (57 shorter events, 2.0 us)
Async XLA Ops:
  35.5 4.9 %copy-start.4 = (s32[16,56]{1,0:T(8,128)S(1)}, s32[16,56]{1,0:T(8,128)}, u32[]{:S(2)}) copy-start(s32[16,56]{1,0:T(8,128)} %param.12) | copy-start | bytes 10756
  35.6 4.9 %copy-start.6 = (s32[16]{0:T(128)S(1)}, s32[16]{0:T(128)}, u32[]{:S(2)}) copy-start(s32[16]{0:T(128)} %param.11) | copy-start | bytes 196
  35.6 5.1 %copy-start.7 = (s32[16]{0:T(128)S(1)}, s32[16]{0:T(128)}, u32[]{:S(2)}) copy-start(s32[16]{0:T(128)} %param.9) | copy-start | bytes 196
  35.6 5.1 %copy-start.8 = (s32[16]{0:T(128)S(1)}, s32[16]{0:T(128)}, u32[]{:S(2)}) copy-start(s32[16]{0:T(128)} %param.10) | copy-start | bytes 196
  47.9 2.0 %copy-start = (f32[16,440,128]{2,1,0:T(8,128)S(1)}, f32[16,440,128]{2,1,0:T(8,128)}, u32[]{:S(2)}) copy-start(f32[16,440,128]{2,1,0:T(8,128)} %get-tuple-element.6) | copy-start | bytes 10813444
  49.9 2.2 %copy-start.3 = (bf16[56,1024]{1,0:T(8,128)(2,1)S(1)}, bf16[56,1024]{1,0:T(8,128)(2,1)}, u32[]{:S(2)}) copy-start(bf16[56,1024]{1,0:T(8,128)(2,1)} %param.14) | copy-start | bytes 344068
  52.1 3.7 %copy-start.1 = (bf16[16,440,64]{2,1,0:T(8,128)(2,1)}, bf16[16,440,64]{2,1,0:T(8,128)(2,1)S(1)}, u32[]{:S(2)}) copy-start(bf16[16,440,64]{2,1,0:T(8,128)(2,1)S(1)} %get-tuple-element.5) | copy-start | bytes 2703364
  59.0 4.8 %copy-start.5 = (s32[1536]{0:T(1024)S(1)}, s32[1536]{0:T(1024)}, u32[]{:S(2)}) copy-start(s32[1536]{0:T(1024)} %param.13) | copy-start | bytes 18436
  65.1 4.4 %copy-start.2 = (bf16[16,440,64]{2,1,0:T(8,128)(2,1)S(1)}, bf16[16,440,64]{2,1,0:T(8,128)(2,1)}, u32[]{:S(2)}) copy-start(bf16[16,440,64]{2,1,0:T(8,128)(2,1)} %copy-done.1) | copy-start | bytes 2703364

commit v3 on v2

--- a/solution.py
+++ b/solution.py
@@ -174,6 +174,102 @@
     )(block)
 
 
+def blend_kernel(
+    all_ref, turn_ref, key_pos_ref, query_ref, query_pos_ref, token_ref,
+    attended_ref, pages_ref, peak_ref, sum_ref, mixed_ref, page_ref,
+):
+    step = pl.program_id(0)
+    together, unit, width = all_ref.shape
+    head_dim = width // 2
+    half_dim = head_dim // 2
+    count = together * unit
+
+    @pl.when(step == 0)
+    def _():
+        peak_ref[...] = jnp.full(peak_ref.shape, -1e30, jnp.float32)
+        sum_ref[...] = jnp.zeros(sum_ref.shape, jnp.float32)
+        mixed_ref[...] = jnp.zeros(mixed_ref.shape, jnp.float32)
+        page_ref[...] = jnp.zeros(page_ref.shape, jnp.float32)
+
+    rows = all_ref[...].reshape(count, width)
+    raw = rows[:, :head_dim].astype(jnp.float32)
+    values = rows[:, head_dim:]
+    turn = turn_ref[...].reshape(count, head_dim)
+    turned = pltpu.roll(turn, half_dim, 1)
+    first = lax.broadcasted_iota(jnp.int32, (count, head_dim), 1) < half_dim
+    cosine = jnp.where(first, turn, turned)
+    sine = jnp.where(first, -turned, turn)
+    keys = (raw * cosine + pltpu.roll(raw, half_dim, 1) * sine).astype(jnp.bfloat16)
+
+    scores = lax.dot_general(
+        query_ref[...], keys, (((1,), (1,)), ((), ())), preferred_element_type=jnp.float32
+    ) * (head_dim ** (-0.5))
+    scores = jnp.where(key_pos_ref[0] <= query_pos_ref[...], scores, -1e30)
+    old_peak = peak_ref[...]
+    peak = jnp.maximum(old_peak, jnp.max(scores, axis=1, keepdims=True))
+    shrink = jnp.exp(old_peak - peak)
+    weights = jnp.exp(scores - peak)
+    peak_ref[...] = peak
+    sum_ref[...] = sum_ref[...] * shrink + jnp.sum(weights, axis=1, keepdims=True)
+    mixed_ref[...] = mixed_ref[...] * shrink + jnp.dot(
+        weights.astype(jnp.bfloat16), values, preferred_element_type=jnp.float32
+    )
+
+    local = token_ref[...] - step * count
+    lanes = lax.broadcasted_iota(jnp.int32, (token_ref.shape[0], count), 1)
+    choose = jnp.where(lanes == local, 1.0, 0.0).astype(jnp.bfloat16)
+    page_ref[:, :head_dim] += jnp.dot(choose, keys, preferred_element_type=jnp.float32)
+    page_ref[:, head_dim:] += jnp.dot(choose, values, preferred_element_type=jnp.float32)
+
+    @pl.when(step == pl.num_programs(0) - 1)
+    def _():
+        attended_ref[...] = (mixed_ref[...] / sum_ref[...]).astype(jnp.bfloat16)
+        pages_ref[...] = page_ref[...].astype(jnp.bfloat16)
+
+
+def blend(everything, turn, key_pos, queries, query_pos, tokens):
+    count, unit, width = everything.shape
+    head_dim = width // 2
+    together = 4
+    steps = count // together
+    query_count = queries.shape[0]
+    token_count = tokens.shape[0]
+
+    def whole(shape):
+        return pl.BlockSpec(shape, lambda i: (0, 0))
+
+    return pl.pallas_call(
+        blend_kernel,
+        grid=(steps,),
+        out_shape=(
+            jax.ShapeDtypeStruct((query_count, head_dim), jnp.bfloat16),
+            jax.ShapeDtypeStruct((token_count, width), jnp.bfloat16),
+        ),
+        in_specs=[
+            pl.BlockSpec((together, unit, width), lambda i: (i, 0, 0)),
+            pl.BlockSpec((together, unit, head_dim), lambda i: (i, 0, 0)),
+            pl.BlockSpec((1, 1, together * unit), lambda i: (i, 0, 0)),
+            whole((query_count, head_dim)),
+            whole((query_count, 1)),
+            whole((token_count, 1)),
+        ],
+        out_specs=(whole((query_count, head_dim)), whole((token_count, width))),
+        scratch_shapes=[
+            pltpu.VMEM((query_count, 1), jnp.float32),
+            pltpu.VMEM((query_count, 1), jnp.float32),
+            pltpu.VMEM((query_count, head_dim), jnp.float32),
+            pltpu.VMEM((token_count, width), jnp.float32),
+        ],
+    )(
+        everything,
+        turn,
+        key_pos.reshape(steps, 1, together * unit),
+        queries,
+        query_pos[:, None],
+        tokens[:, None],
+    )
+
+
 def pick(one_hot, table):
     return jnp.dot(one_hot.astype(jnp.float32), table, precision=lax.Precision.HIGHEST)
 
@@ -192,11 +288,26 @@
     total_pages = seq_count * page_count
     bf16 = jnp.bfloat16
 
-    unit = tok_count + sel_count
-    block = jnp.concatenate([pool_kv.reshape(tok_count, 2 * head_dim), fresh_kv], axis=0)
+    filled = tok_count + sel_count
+    unit = -(-filled // 64) * 64
+    far = jnp.int32(2**30)
+
+    passage_ids = jnp.arange(seq_count, dtype=jnp.int32)
+    mine = (passage_ids == my_index)[:, None]
+    picked = jnp.sum(jnp.where(mine, recompute_pos, 0), axis=0)
+    start_pos = jnp.sum(jnp.where(mine[:, 0], passage_start, 0))
+    fresh_pos = start_pos + picked
+    fresh_keys = rotate_pos(fresh_kv[:, :head_dim].astype(jnp.float32), fresh_pos).astype(bf16)
+    block = jnp.concatenate(
+        [
+            pool_kv.reshape(tok_count, 2 * head_dim),
+            jnp.concatenate([fresh_keys, fresh_kv[:, head_dim:]], axis=1),
+            jnp.zeros((unit - filled, 2 * head_dim), bf16),
+        ],
+        axis=0,
+    )
     everything = spread(block, seq_count)
 
-    passage_ids = jnp.arange(seq_count, dtype=jnp.int32)
     placed = passage_order[:, None] == passage_ids[None, :]
     slots = jnp.sum(jnp.where(placed, pool_slot[None, :], 0), axis=1)
 
@@ -218,32 +329,23 @@
     replaced = jnp.any(
         row_recompute[:, None, :] == row_tok[:, :, None].astype(jnp.float32), axis=2
     )
-    far = jnp.int32(2**30)
     cached_pos = jnp.where(replaced, far, row_passage[:, None] * tok_count + row_tok).reshape(-1)
     fresh_place = passage_ids[:, None] * tok_count + recompute_pos
-    key_pos = jnp.concatenate([cached_pos.reshape(seq_count, tok_count), fresh_place], axis=1)
-    key_pos = key_pos.reshape(-1)
-
-    fresh_angles = (passage_start[:, None] + recompute_pos).astype(jnp.float32)[
-        :, :, None
-    ] * frequency
-    fresh_turn = jnp.concatenate([jnp.cos(fresh_angles), jnp.sin(fresh_angles)], axis=-1)
+    key_pos = jnp.concatenate(
+        [
+            cached_pos.reshape(seq_count, tok_count),
+            fresh_place,
+            jnp.full((seq_count, unit - filled), far, jnp.int32),
+        ],
+        axis=1,
+    )
     cached_turn = jnp.broadcast_to(
         row_turn.reshape(seq_count, page_count, 1, head_dim),
         (seq_count, page_count, PAGE, head_dim),
     ).reshape(seq_count, tok_count, head_dim)
+    still = jnp.where(jnp.arange(head_dim) < half_dim, 1.0, 0.0).astype(jnp.float32)
+    fresh_turn = jnp.broadcast_to(still, (seq_count, unit - tok_count, head_dim))
     turn = jnp.concatenate([cached_turn, fresh_turn], axis=1)
-    raw = everything[:, :, :head_dim].astype(jnp.float32)
-    cosine = turn[:, :, :half_dim]
-    sine = turn[:, :, half_dim:]
-    lower = raw[:, :, :half_dim]
-    upper = raw[:, :, half_dim:]
-    keys = (
-        jnp.concatenate([lower * cosine - upper * sine, upper * cosine + lower * sine], axis=-1)
-        .astype(bf16)
-        .reshape(seq_count * unit, head_dim)
-    )
-    values = everything[:, :, head_dim:].reshape(seq_count * unit, head_dim)
 
     my_rows = my_index * page_count + jnp.arange(page_count, dtype=jnp.int32)
     source = jnp.sum(
@@ -271,37 +373,16 @@
         source_passage[:, None] * unit + tok_count + sel_at - 1,
         source_row[:, None] + lane[None, :],
     ).reshape(-1)
-    choose = (
-        token_at[:, None] == jnp.arange(seq_count * unit, dtype=jnp.int32)[None, :]
-    ).astype(bf16)
-    page_keys = jnp.dot(choose, keys, preferred_element_type=jnp.float32).astype(bf16)
-    page_values = jnp.dot(choose, values, preferred_element_type=jnp.float32).astype(bf16)
-    decode_cache = jnp.concatenate([page_keys, page_values], axis=1).reshape(
-        page_count, row_width
-    )
-
-    mine = (passage_ids == my_index)[:, None]
-    picked = jnp.sum(jnp.where(mine, recompute_pos, 0), axis=0)
-    start_pos = jnp.sum(jnp.where(mine[:, 0], passage_start, 0))
     queries = rotate_pos(
-        fresh_q.reshape(sel_count, GROUP, head_dim).astype(jnp.float32),
-        (start_pos + picked)[:, None],
+        fresh_q.reshape(sel_count, GROUP, head_dim).astype(jnp.float32), fresh_pos[:, None]
     ).astype(bf16)
     query_rows = queries.reshape(-1, head_dim)
     query_pos = jnp.repeat(my_index * tok_count + picked, GROUP)
-    attended = attend(query_rows, query_pos, keys, values, key_pos)
-    return (attended.reshape(sel_count, GROUP * head_dim), decode_cache)
-
-
-def attend(query_rows, query_pos, keys, values, key_pos):
-    score_scale = keys.shape[1] ** (-0.5)
-    scores = jnp.dot(query_rows, keys.T, preferred_element_type=jnp.float32) * score_scale
-    allowed = key_pos[None, :] <= query_pos[:, None]
-    peak = jnp.max(jnp.where(allowed, scores, -jnp.inf), axis=1)
-    weights = jnp.where(allowed, jnp.exp(scores - peak[:, None]), 0.0)
-    weight_sum = jnp.sum(weights, axis=1)
-    weighted = jnp.dot(weights.astype(jnp.bfloat16), values, preferred_element_type=jnp.float32)
-    return (weighted / weight_sum[:, None]).astype(jnp.bfloat16)
+    attended, pages = blend(everything, turn, key_pos, query_rows, query_pos, token_at)
+    return (
+        attended.reshape(sel_count, GROUP * head_dim),
+        pages.reshape(page_count, row_width),
+    )
 
 
 def solution(mesh):

time: 74 us -> 70.7 us (0.955)
  Pallas kernels: 32.4 us -> 47 us
  matrix products: 16.3 us -> 2.12 us
  other arithmetic: 16.6 us -> 11.1 us
  local copies, waits for them, and re-layouts: 7.36 us -> 9.12 us
    dot_general x4 -> x0, matrix products: 14.9 us -> none  [the longest x1 4.37 us: shards(): jnp.dot(choose, values, preferred_element_type=jnp.float32).astype(bf16)]
    pallas_call x0 -> x1, Pallas kernels: none -> 14.3 us  [blend(): pl.pallas_call(blend_kernel, grid=(steps,), out_shape=(jax.ShapeDtypeStru...]
    reduce_sum x2 -> x0, other arithmetic: 3.73 us -> none  [the longest x1 3.1 us: attend(): weight_sum = jnp.sum(weights, axis=1)]
    convert_element_type x1 -> x2, other arithmetic: 4.84 us -> 2.11 us  [the longest x1 1.37 us: shards(): start_angles = passage_start.astype(jnp.float32)[:, None] * frequency]
    reshape x2 -> x3, local copies, waits for them, and re-layouts: 1.5 us -> 4.02 us  [the longest x1 1.73 us: shards(): pages.reshape(page_count, row_width)]
    another operation x1 -> x0, other arithmetic: 2.19 us -> none
    concatenate x1, other arithmetic: 0.34 us -> 2.16 us  [shards(): turn = jnp.concatenate([cached_turn, fresh_turn], axis=1)]
    unnamed x19 -> x3, local copies, waits for them, and re-layouts: 1.75 us -> 0.05 us
where the time goes in v3:
time: 70.7 us; the launch traced here: 70.3 us
  Pallas kernels  47 us (66%)
  other arithmetic  11.1 us (16%)
  local copies, waits for them, and re-layouts  9.12 us (13%)
  matrix products  2.12 us (3%)
  between operations  0.85 us (1%)
    pallas_call x1, Pallas kernels, spread(): pl.pallas_call(lambda *refs: spread_kernel(count, *refs), out_shape=jax.S...  32.7 us
    pallas_call x1, Pallas kernels, blend(): pl.pallas_call(blend_kernel, grid=(steps,), out_shape=(jax.ShapeDtypeStru...  14.3 us
    concatenate x1, other arithmetic, shards(): turn = jnp.concatenate([cached_turn, fresh_turn], axis=1)  2.16 us
    dot_general x3, matrix products, pick(): jnp.dot(one_hot.astype(jnp.float32), table, precision=lax.Precision.HIGHEST)  2.12 us
    reshape x1, local copies, waits for them, and re-layouts, shards(): pages.reshape(page_count, row_width)  1.73 us
    reshape x1, local copies, waits for them, and re-layouts, shards(): attended.reshape(sel_count, GROUP * head_dim)  1.6 us

profile of v3, /device:TPU:0, one launch (start us, length us, event | category | flops | bytes accessed | tf_op | source)
XLA Modules:
  0.0 70.3 jit_solution(7673387992200449814)
XLA Ops:
  0.7 0.9 %select_reduce_fusion = s32[96]{0:T(128)S(1)} fusion(s32[1536]{0:T(1024)} %param.13, s32[96]{0:T(128)S(1)} %iota_add_fusion.1), kind=kLoop, calls=%fused_computation.2 | loop fusion | flops 442272 | bytes 6912 | tf_op jit(solution)/shard_map/reduce_sum | solution.py:351
  1.6 0.9 %select_reduce_fusion.3 = s32[16]{0:T(128)S(1)} fusion(s32[16]{0:T(128)} %param.9, s32[16]{0:T(128)} %param.10), kind=kLoop, calls=%fused_computation.69 | loop fusion | flops 752 | bytes 192 | tf_op jit(solution)/shard_map/reduce_sum | solution.py:312
  2.6 1.4 %fusion.41 = (f32[16]{0:T(128)S(1)}, s32[]{:T(128)}) fusion(s32[16]{0:T(128)} %param.11, s32[]{:T(128)S(6)} %axis_index.12), kind=kLoop, calls=%fused_computation.101 | loop fusion | flops 63 | bytes 136 | tf_op jit(solution)/shard_map/convert_element_type | solution.py:315
  4.2 0.8 %broadcast_add_fusion = (s32[16,56]{1,0:T(8,128)S(1)}, s32[56]{0:T(128)S(1)}) fusion(s32[16,56]{1,0:T(8,128)} %param.12, s32[16]{0:T(128)S(1)} %iota_multiply_fusion, pred[16]{0:T(512)(128)(4,1)S(1)} %iota_compare_fusion.3), kind=kLoop, calls=%fused_computation.76 | loop fusion | flops 2632 | bytes 7472 | tf_op jit(solution)/shard_map/add | solution.py:333
  4.9 0.6 broadcast_add_fusion.1
  5.6 0.1 fusion.6
  5.8 0.1 multiply_cosine_fusion.1
  6.0 0.9 %fusion.33 = f32[96,56]{0,1:T(8,128)S(1)} fusion(s32[16,56]{1,0:T(8,128)} %param.12, s32[96]{0:T(128)S(1)} %get-tuple-element.7), kind=kOutput, calls=%fused_computation.66 | convolution fusion | flops 1034624 | bytes 25472 | tf_op jit(solution)/shard_map/dot_general | solution.py:274
  7.0 0.1 select_reduce_fusion.1
  7.2 0.7 %slice_convert_fusion = (f32[56,128]{1,0:T(8,128)S(1)}, bf16[56,128]{1,0:T(8,128)(2,1)S(1)}) fusion(bf16[56,256]{1,0:T(8,128)(2,1)} %param.15), kind=kLoop, calls=%fused_computation.49 | loop fusion | flops 7168 | bytes 71680 | tf_op jit(solution)/shard_map/convert_element_type | solution.py:300
  7.9 0.1 copy.29
  8.1 0.1 add.297
  8.2 0.2 multiply_cosine_fusion
  8.5 0.8 %select_n.167.token_ref = s32[384,1]{1,0:T(8,128)} reshape(s32[96,4]{1,0:T(8,128)S(1)} %copy.29) | data formatting | bytes 3072 | tf_op jit(solution)/shard_map/jit(_where)/select_n | solution.py:371
  9.5 1.1 %reshape.352 = bf16[384,256]{1,0:T(8,128)(2,1)S(1)} reshape(bf16[96,1024]{1,0:T(8,128)(2,1)} %param.8) | data formatting | bytes 393216 | tf_op jit(solution)/shard_map/reshape | solution.py:303
  10.5 0.8 %maximum_maximum_fusion.refs_0_ = bf16[448,256]{1,0:T(8,128)(2,1)} fusion(bf16[56,128]{1,0:T(8,128)(2,1)S(1)} %get-tuple-element.13, bf16[56,64]{1,0:T(8,128)(2,1)S(1)} %get-tuple-element.18, bf16[56,64]{1,0:T(8,128)(2,1)S(1)} %get-tuple-element.19, bf16[384,256]{1,0:T(8,128)(2,1)S(1)} %reshape.352, bf16[448]{0:T(512)(128)(2,1)S(1)} %pad.13.clone), kind=kLoop, calls=%fused_computation.3 | loop fusion | flops 1146880 | bytes 455552 | tf_op jit(solution)/shard_map/concatenate | solution.py:301
  11.4 0.8 %broadcast_in_dim_reshape.5.query_pos_ref = s32[448,1]{1,0:T(8,128)} reshape(s32[56,8]{1,0:T(8,128)S(1)} %broadcast_in_dim.156) | data formatting | bytes 3584 | tf_op jit(solution)/shard_map/broadcast_in_dim;reshape | solution.py:268
  12.2 0.9 %convert_bitcast_fusion = f32[7,8,8,128]{3,1,2,0:T(8,128)S(1)} fusion(bf16[56,1024]{1,0:T(8,128)(2,1)} %param.14), kind=kLoop, calls=%fused_computation.4 | loop fusion | flops 57344 | bytes 344064
  13.1 0.1 fusion.4
  13.3 0.8 %pad_maximum_fusion.1.query_ref = bf16[448,128]{1,0:T(8,128)(2,1)} fusion(bf16[448,64]{1,0:T(8,128)(2,1)S(1)} %get-tuple-element.9, bf16[448,64]{1,0:T(8,128)(2,1)S(1)} %get-tuple-element.8), kind=kLoop, calls=%fused_computation.14 | loop fusion | flops 229376 | bytes 229376 | tf_op jit(solution)/shard_map/concatenate | solution.py:23
  14.0 0.3 fusion
  14.4 0.2 compare_reduce_fusion
  14.6 0.4 copy.25
  15.0 0.5 reduce_or.12
  15.6 0.7 reshape.354.key_pos_ref
  16.3 0.9 %fusion.2 = f32[1536,128]{1,0:T(8,128)S(1)} fusion(s32[1536]{0:T(1024)S(1)} %add_select_fusion.5, s32[16]{0:T(128)S(1)} %select_reduce_fusion.3, f32[16,64]{1,0:T(8,128)S(1)} %get-tuple-element.21, f32[16,64]{1,0:T(8,128)S(1)} %get-tuple-element.20), kind=kOutput, calls=%fused_computation.10 | convolution fusion | flops 37775360 | bytes 800832 | tf_op jit(solution)/shard_map/dot_general | solution.py:274
  17.2 0.5 broadcast_in_dim.148
  17.7 2.2 %pad_maximum_fusion.turn_ref = f32[16,448,128]{2,1,0:T(8,128)} fusion(f32[16,64,128]{2,1,0:T(8,128)S(1)} %broadcast_in_dim.151, f32[16,384,128]{2,1,0:T(8,128)S(1)} %bitcast.11), kind=kLoop, calls=%fused_computation | loop fusion | flops 917504 | bytes 7340032 | tf_op jit(solution)/shard_map/concatenate | solution.py:348
  19.9 32.7 %shard_map.95.all_ref = bf16[16,448,256]{2,1,0:T(8,128)(2,1)} custom-call(bf16[448,256]{1,0:T(8,128)(2,1)} %maximum_maximum_fusion.refs_0_), custom_call_target="tpu_custom_call" | custom-call | tf_op jit(solution)/shard_map/pallas_call | solution.py:163
  52.7 14.3 %shard_map.96 = (bf16[448,128]{1,0:T(8,128)(2,1)}, bf16[384,256]{1,0:T(8,128)(2,1)}) custom-call(bf16[16,448,256]{2,1,0:T(8,128)(2,1)} %shard_map.95.all_ref, f32[16,448,128]{2,1,0:T(8,128)} %pad_maximum_fusion.turn_ref, s32[4,1,1792]{2,1,0:T(1,128)} %reshape.354.key_pos_ref, bf16[448,128]{1,0:T(8,128)(2,1)} %pad_maximum_fusion.1.query_ref, ...), custom_call_target="tpu_custom_call" | custom-call | tf_op jit(solution)/shard_map/pallas_call | solution.py:241
  66.9 1.6 %reshape.355 = bf16[56,1024]{1,0:T(8,128)(2,1)} reshape(bf16[448,128]{1,0:T(8,128)(2,1)} %get-tuple-element.4) | data formatting | bytes 229376 | tf_op jit(solution)/shard_map/reshape | solution.py:383
  68.5 1.7 %reshape.356 = bf16[96,1024]{1,0:T(8,128)(2,1)} reshape(bf16[384,256]{1,0:T(8,128)(2,1)} %get-tuple-element.5) | data formatting | bytes 393216 | tf_op jit(solution)/shard_map/reshape | solution.py:384
  (34 shorter events, 1.1 us)
Async XLA Ops:
  0.6 13.4 %copy-start = (s32[16,56]{1,0:T(8,128)S(1)}, s32[16,56]{1,0:T(8,128)}, u32[]{:S(2)}) copy-start(s32[16,56]{1,0:T(8,128)} %param.12) | copy-start | bytes 10756

commit v4 on v3

--- a/solution.py
+++ b/solution.py
@@ -10,6 +10,7 @@
 
 
 ROPE_BASE = 500000.0
+LOG2_E = 1.4426950408889634
 
 
 def rotate_pos(vector, positions):
@@ -30,9 +31,10 @@
 
 def spread_kernel(count, block_ref, all_ref, send_sem, recv_sem, own_sem):
     rows = block_ref.shape[0]
-    cut = rows * 3 // 5 // 16 * 16
+    length = count // 4
+    halves = max(2, 2 * (length - 1))
+    cut = rows * (halves - 1) // halves // 16 * 16
     parts = (pl.ds(0, cut), pl.ds(cut, rows - cut))
-    length = count // 4
     me = lax.axis_index("seq")
     at = me // 4
     inner = lax.rem(me, 4)
@@ -91,11 +93,11 @@
         act(1, across, 3, sibling)
 
     def each(step, act, wait):
-        for way, exists, more, device, place in (
-            (0, at - step >= 0, has_up, up, at - step),
-            (1, at + step < length, has_down, down, at + step),
-        ):
-            for part, where, cross in ((0, inner, True), (1, inner, False), (1, across_inner, False)):
+        for part, where, cross in ((0, inner, True), (1, inner, False), (1, across_inner, False)):
+            for way, exists, more, device, place in (
+                (0, at - step >= 0, has_up, up, at - step),
+                (1, at + step < length, has_down, down, at + step),
+            ):
                 block = place * 4 + where
 
                 @pl.when(exists)
@@ -129,12 +131,13 @@
     @pl.loop(1, length)
     def _(step):
         each(step, begin, True)
-
-    crossed_here(begin, True)
-
-    @pl.loop(1, length)
-    def _(step):
-        crossed(step, begin, True)
+        pl.when(step == 1)(lambda: crossed_here(begin, True))
+        pl.when(step > 1)(lambda: crossed(step - 1, begin, True))
+
+    if length == 1:
+        crossed_here(begin, True)
+    else:
+        crossed(length - 1, begin, True)
 
     @pl.loop(0, length)
     def _(place):
@@ -176,7 +179,7 @@
 
 def blend_kernel(
     all_ref, turn_ref, key_pos_ref, query_ref, query_pos_ref, token_ref,
-    attended_ref, pages_ref, peak_ref, sum_ref, mixed_ref, page_ref,
+    attended_ref, pages_ref, peak_ref, sum_ref, mixed_ref, page_key_ref, page_value_ref,
 ):
     step = pl.program_id(0)
     together, unit, width = all_ref.shape
@@ -189,12 +192,33 @@
         peak_ref[...] = jnp.full(peak_ref.shape, -1e30, jnp.float32)
         sum_ref[...] = jnp.zeros(sum_ref.shape, jnp.float32)
         mixed_ref[...] = jnp.zeros(mixed_ref.shape, jnp.float32)
-        page_ref[...] = jnp.zeros(page_ref.shape, jnp.float32)
+        page_key_ref[...] = jnp.zeros(page_key_ref.shape, jnp.float32)
+        page_value_ref[...] = jnp.zeros(page_value_ref.shape, jnp.float32)
 
     rows = all_ref[...].reshape(count, width)
     raw = rows[:, :head_dim].astype(jnp.float32)
     values = rows[:, head_dim:]
-    turn = turn_ref[...].reshape(count, head_dim)
+    pages = turn_ref.shape[1]
+    owner = lax.broadcasted_iota(jnp.int32, (unit, pages), 0) // PAGE
+    expand = jnp.where(
+        owner == lax.broadcasted_iota(jnp.int32, (unit, pages), 1), 1.0, 0.0
+    ).astype(jnp.float32)
+    at_row = lax.broadcasted_iota(jnp.int32, (unit, head_dim), 0)
+    at_lane = lax.broadcasted_iota(jnp.int32, (unit, head_dim), 1)
+    still = jnp.where((at_row >= pages * PAGE) & (at_lane < half_dim), 1.0, 0.0)
+    turn = jnp.concatenate(
+        [
+            jnp.dot(
+                expand,
+                turn_ref[part],
+                precision=lax.Precision.HIGHEST,
+                preferred_element_type=jnp.float32,
+            )
+            + still
+            for part in range(together)
+        ],
+        axis=0,
+    )
     turned = pltpu.roll(turn, half_dim, 1)
     first = lax.broadcasted_iota(jnp.int32, (count, head_dim), 1) < half_dim
     cosine = jnp.where(first, turn, turned)
@@ -203,12 +227,13 @@
 
     scores = lax.dot_general(
         query_ref[...], keys, (((1,), (1,)), ((), ())), preferred_element_type=jnp.float32
-    ) * (head_dim ** (-0.5))
+    )
+    slope = head_dim ** (-0.5) * LOG2_E
     scores = jnp.where(key_pos_ref[0] <= query_pos_ref[...], scores, -1e30)
     old_peak = peak_ref[...]
     peak = jnp.maximum(old_peak, jnp.max(scores, axis=1, keepdims=True))
-    shrink = jnp.exp(old_peak - peak)
-    weights = jnp.exp(scores - peak)
+    shrink = jnp.exp2((old_peak - peak) * slope)
+    weights = jnp.exp2((scores - peak) * slope)
     peak_ref[...] = peak
     sum_ref[...] = sum_ref[...] * shrink + jnp.sum(weights, axis=1, keepdims=True)
     mixed_ref[...] = mixed_ref[...] * shrink + jnp.dot(
@@ -218,13 +243,22 @@
     local = token_ref[...] - step * count
     lanes = lax.broadcasted_iota(jnp.int32, (token_ref.shape[0], count), 1)
     choose = jnp.where(lanes == local, 1.0, 0.0).astype(jnp.bfloat16)
-    page_ref[:, :head_dim] += jnp.dot(choose, keys, preferred_element_type=jnp.float32)
-    page_ref[:, head_dim:] += jnp.dot(choose, values, preferred_element_type=jnp.float32)
+    page_key_ref[...] += jnp.dot(choose, keys, preferred_element_type=jnp.float32)
+    page_value_ref[...] += jnp.dot(choose, values, preferred_element_type=jnp.float32)
 
     @pl.when(step == pl.num_programs(0) - 1)
     def _():
-        attended_ref[...] = (mixed_ref[...] / sum_ref[...]).astype(jnp.bfloat16)
-        pages_ref[...] = page_ref[...].astype(jnp.bfloat16)
+        mixed_ref[...] = mixed_ref[...] / sum_ref[...]
+        for head in range(GROUP):
+            attended_ref[:, head * head_dim : (head + 1) * head_dim] = mixed_ref[
+                pl.ds(head, attended_ref.shape[0], stride=GROUP), :
+            ].astype(jnp.bfloat16)
+        for token in range(PAGE):
+            for at, held in enumerate((page_key_ref, page_value_ref)):
+                start = (2 * token + at) * head_dim
+                pages_ref[:, start : start + head_dim] = held[
+                    pl.ds(token, pages_ref.shape[0], stride=PAGE), :
+                ].astype(jnp.bfloat16)
 
 
 def blend(everything, turn, key_pos, queries, query_pos, tokens):
@@ -242,23 +276,27 @@
         blend_kernel,
         grid=(steps,),
         out_shape=(
-            jax.ShapeDtypeStruct((query_count, head_dim), jnp.bfloat16),
-            jax.ShapeDtypeStruct((token_count, width), jnp.bfloat16),
+            jax.ShapeDtypeStruct((query_count // GROUP, GROUP * head_dim), jnp.bfloat16),
+            jax.ShapeDtypeStruct((token_count // PAGE, PAGE * width), jnp.bfloat16),
         ),
         in_specs=[
             pl.BlockSpec((together, unit, width), lambda i: (i, 0, 0)),
-            pl.BlockSpec((together, unit, head_dim), lambda i: (i, 0, 0)),
+            pl.BlockSpec((together, token_count // PAGE, head_dim), lambda i: (i, 0, 0)),
             pl.BlockSpec((1, 1, together * unit), lambda i: (i, 0, 0)),
             whole((query_count, head_dim)),
             whole((query_count, 1)),
             whole((token_count, 1)),
         ],
-        out_specs=(whole((query_count, head_dim)), whole((token_count, width))),
+        out_specs=(
+            whole((query_count // GROUP, GROUP * head_dim)),
+            whole((token_count // PAGE, PAGE * width)),
+        ),
         scratch_shapes=[
             pltpu.VMEM((query_count, 1), jnp.float32),
             pltpu.VMEM((query_count, 1), jnp.float32),
             pltpu.VMEM((query_count, head_dim), jnp.float32),
-            pltpu.VMEM((token_count, width), jnp.float32),
+            pltpu.VMEM((token_count, head_dim), jnp.float32),
+            pltpu.VMEM((token_count, head_dim), jnp.float32),
         ],
     )(
         everything,
@@ -280,7 +318,6 @@
     seq_count = lax.axis_size("seq")
     my_index = lax.axis_index("seq")
     page_count = pool_kv.shape[0]
-    row_width = pool_kv.shape[1]
     head_dim = fresh_kv.shape[1] // 2
     half_dim = head_dim // 2
     sel_count = fresh_q.shape[0]
@@ -339,13 +376,7 @@
         ],
         axis=1,
     )
-    cached_turn = jnp.broadcast_to(
-        row_turn.reshape(seq_count, page_count, 1, head_dim),
-        (seq_count, page_count, PAGE, head_dim),
-    ).reshape(seq_count, tok_count, head_dim)
-    still = jnp.where(jnp.arange(head_dim) < half_dim, 1.0, 0.0).astype(jnp.float32)
-    fresh_turn = jnp.broadcast_to(still, (seq_count, unit - tok_count, head_dim))
-    turn = jnp.concatenate([cached_turn, fresh_turn], axis=1)
+    turn = row_turn.reshape(seq_count, page_count, head_dim)
 
     my_rows = my_index * page_count + jnp.arange(page_count, dtype=jnp.int32)
     source = jnp.sum(
@@ -379,10 +410,7 @@
     query_rows = queries.reshape(-1, head_dim)
     query_pos = jnp.repeat(my_index * tok_count + picked, GROUP)
     attended, pages = blend(everything, turn, key_pos, query_rows, query_pos, token_at)
-    return (
-        attended.reshape(sel_count, GROUP * head_dim),
-        pages.reshape(page_count, row_width),
-    )
+    return (attended, pages)
 
 
 def solution(mesh):

time: 70.7 us -> 63.8 us (0.902)
  local copies, waits for them, and re-layouts: 9.12 us -> 4.29 us
  other arithmetic: 11.1 us -> 8.17 us
  matrix products: 2.12 us -> 3.01 us
    reshape x2 -> x0, local copies, waits for them, and re-layouts: 3.32 us -> none  [the longest x1 1.73 us: shards(): pages.reshape(page_count, row_width)]
    concatenate x1 -> x0, other arithmetic: 2.16 us -> none  [shards(): turn = jnp.concatenate([cached_turn, fresh_turn], axis=1)]
    pallas_call x1, Pallas kernels: 14.3 us -> 16.3 us  [blend(): pl.pallas_call(blend_kernel, grid=(steps,), out_shape=(jax.ShapeDtypeStru...]
    pallas_call x1, Pallas kernels: 32.7 us -> 30.8 us  [spread(): pl.pallas_call(lambda *refs: spread_kernel(count, *refs), out_shape=jax.S...]
    reshape x1, local copies, waits for them, and re-layouts: 1.08 us -> 0.15 us  [shards(): pool_kv.reshape(tok_count, 2 * head_dim)]
    unnamed x1, other arithmetic: 0.91 us -> 0.02 us
    dot_general x3, matrix products: 2.12 us -> 3.01 us  [pick(): jnp.dot(one_hot.astype(jnp.float32), table, precision=lax.Precision.HIGHEST)]
where the time goes in v4:
time: 63.8 us; the launch traced here: 63.4 us
  Pallas kernels  47.1 us (74%)
  other arithmetic  8.17 us (13%)
  local copies, waits for them, and re-layouts  4.29 us (7%)
  matrix products  3.01 us (5%)
  between operations  0.85 us (1%)
    pallas_call x1, Pallas kernels, spread(): pl.pallas_call(lambda *refs: spread_kernel(count, *refs), out_shape=jax.S...  30.8 us
    pallas_call x1, Pallas kernels, blend(): pl.pallas_call(blend_kernel, grid=(steps,), out_shape=(jax.ShapeDtypeStru...  16.3 us
    dot_general x3, matrix products, pick(): jnp.dot(one_hot.astype(jnp.float32), table, precision=lax.Precision.HIGHEST)  3.01 us
    convert_element_type x1, other arithmetic, shards(): start_angles = passage_start.astype(jnp.float32)[:, None] * frequency  1.37 us

profile of v4, /device:TPU:0, one launch (start us, length us, event | category | flops | bytes accessed | tf_op | source)
XLA Modules:
  0.0 63.4 jit_solution(4477070211281132354)
XLA Ops:
  0.7 1.0 %select_reduce_fusion = s32[96]{0:T(128)S(1)} fusion(s32[1536]{0:T(1024)} %param.13, s32[96]{0:T(128)S(1)} %iota_add_fusion.1), kind=kLoop, calls=%fused_computation.1 | loop fusion | flops 442272 | bytes 6912 | tf_op jit(solution)/shard_map/reduce_sum | solution.py:382
  1.6 0.9 %select_reduce_fusion.3 = s32[16]{0:T(128)S(1)} fusion(s32[16]{0:T(128)} %param.9, s32[16]{0:T(128)} %param.10), kind=kLoop, calls=%fused_computation.68 | loop fusion | flops 752 | bytes 192 | tf_op jit(solution)/shard_map/reduce_sum | solution.py:349
  2.6 1.4 %fusion.41 = (f32[16]{0:T(128)S(1)}, s32[]{:T(128)}) fusion(s32[16]{0:T(128)} %param.11, s32[]{:T(128)S(6)} %axis_index.12), kind=kLoop, calls=%fused_computation.99 | loop fusion | flops 63 | bytes 136 | tf_op jit(solution)/shard_map/convert_element_type | solution.py:352
  4.0 0.1 select_reduce_fusion.2
  4.2 0.8 %broadcast_add_fusion = (s32[16,56]{1,0:T(8,128)S(1)}, s32[56]{0:T(128)S(1)}) fusion(s32[16,56]{1,0:T(8,128)} %param.12, s32[16]{0:T(128)S(1)} %iota_multiply_fusion, pred[16]{0:T(512)(128)(4,1)S(1)} %iota_compare_fusion.3), kind=kLoop, calls=%fused_computation.75 | loop fusion | flops 2632 | bytes 7472 | tf_op jit(solution)/shard_map/add | solution.py:370
  5.0 0.6 %broadcast_add_fusion.1 = (s32[56]{0:T(128)S(1)}, f32[56]{0:T(128)S(1)}) fusion(s32[56]{0:T(128)S(1)} %get-tuple-element.11, s32[]{:T(128)S(6)} %mul.235, s32[]{:T(128)} %get-tuple-element.23), kind=kLoop, calls=%fused_computation.97 | loop fusion | flops 168 | bytes 680 | tf_op jit(solution)/shard_map/add | solution.py:411
  5.7 0.1 fusion.6
  5.9 0.1 multiply_cosine_fusion.1
  6.1 0.9 %fusion.33 = f32[96,56]{0,1:T(8,128)S(1)} fusion(s32[16,56]{1,0:T(8,128)} %param.12, s32[96]{0:T(128)S(1)} %get-tuple-element.3), kind=kOutput, calls=%fused_computation.65 | convolution fusion | flops 1034624 | bytes 25472 | tf_op jit(solution)/shard_map/dot_general | solution.py:312
  7.0 0.1 select_reduce_fusion.1
  7.1 0.1 copy.26
  7.2 0.8 %slice_convert_fusion = (f32[56,128]{1,0:T(8,128)S(1)}, bf16[56,128]{1,0:T(8,128)(2,1)S(1)}) fusion(bf16[56,256]{1,0:T(8,128)(2,1)} %param.15), kind=kLoop, calls=%fused_computation.48 | loop fusion | flops 7168 | bytes 71680 | tf_op jit(solution)/shard_map/convert_element_type | solution.py:337
  8.0 0.1 copy.29
  8.1 0.1 fusion.10
  8.2 0.1 add.297
  8.3 0.2 multiply_cosine_fusion
  8.5 0.1 copy.27
  8.6 0.8 %select_n.162.token_ref = s32[384,1]{1,0:T(8,128)} reshape(s32[96,4]{1,0:T(8,128)S(1)} %copy.29) | data formatting | bytes 3072 | tf_op jit(solution)/shard_map/jit(_where)/select_n | solution.py:402
  9.5 0.1 copy.28
  9.6 0.1 reshape.344
  9.7 0.8 %maximum_maximum_fusion.refs_0_ = bf16[448,256]{1,0:T(8,128)(2,1)} fusion(bf16[56,128]{1,0:T(8,128)(2,1)S(1)} %get-tuple-element.9, bf16[56,64]{1,0:T(8,128)(2,1)S(1)} %get-tuple-element.14, bf16[56,64]{1,0:T(8,128)(2,1)S(1)} %get-tuple-element.15, bf16[384,256]{1,0:T(8,128)(2,1)S(1)} %reshape.344, bf16[448]{0:T(512)(128)(2,1)S(1)} %pad.11.clone), kind=kLoop, calls=%fused_computation.2 | loop fusion | flops 1146880 | bytes 455552 | tf_op jit(solution)/shard_map/concatenate | solution.py:338
  10.5 0.8 %broadcast_in_dim_reshape.5.query_pos_ref = s32[448,1]{1,0:T(8,128)} reshape(s32[56,8]{1,0:T(8,128)S(1)} %broadcast_in_dim.133) | data formatting | bytes 3584 | tf_op jit(solution)/shard_map/broadcast_in_dim;reshape | solution.py:306
  11.4 0.1 fusion.4
  11.6 0.8 %pad_maximum_fusion.query_ref = bf16[448,128]{1,0:T(8,128)(2,1)} fusion(bf16[448,64]{1,0:T(8,128)(2,1)S(1)} %get-tuple-element.5, bf16[448,64]{1,0:T(8,128)(2,1)S(1)} %get-tuple-element.4), kind=kLoop, calls=%fused_computation.13 | loop fusion | flops 229376 | bytes 229376 | tf_op jit(solution)/shard_map/concatenate | solution.py:24
  12.3 0.3 fusion
  12.7 0.2 compare_reduce_fusion
  12.9 0.4 copy.25
  13.3 0.5 reduce_or.12
  13.8 0.7 %reshape.346.key_pos_ref = s32[4,1,1792]{2,1,0:T(1,128)} reshape(s32[16,448]{1,0:T(8,128)S(1)} %add_add_fusion) | data formatting | bytes 57344 | tf_op jit(solution)/shard_map/reshape | solution.py:304
  14.5 1.8 %fusion.2 = f32[1536,128]{1,0:T(8,128)} fusion(s32[1536]{0:T(1024)S(1)} %add_select_fusion.5, s32[16]{0:T(128)S(1)} %select_reduce_fusion.3, f32[16,64]{1,0:T(8,128)S(1)} %get-tuple-element.17, f32[16,64]{1,0:T(8,128)S(1)} %get-tuple-element.16), kind=kOutput, calls=%fused_computation.9 | convolution fusion | flops 37775360 | bytes 800832 | tf_op jit(solution)/shard_map/dot_general | solution.py:312
  16.3 30.8 %shard_map.95.all_ref = bf16[16,448,256]{2,1,0:T(8,128)(2,1)} custom-call(bf16[448,256]{1,0:T(8,128)(2,1)} %maximum_maximum_fusion.refs_0_), custom_call_target="tpu_custom_call" | custom-call | tf_op jit(solution)/shard_map/pallas_call | solution.py:166
  47.1 16.3 %shard_map.96 = (bf16[56,1024]{1,0:T(8,128)(2,1)}, bf16[96,1024]{1,0:T(8,128)(2,1)}) custom-call(bf16[16,448,256]{2,1,0:T(8,128)(2,1)} %shard_map.95.all_ref, f32[16,96,128]{2,1,0:T(8,128)} %bitcast.10, s32[4,1,1792]{2,1,0:T(1,128)} %reshape.346.key_pos_ref, bf16[448,128]{1,0:T(8,128)(2,1)} %pad_maximum_fusion.query_ref, ...), custom_call_target="tpu_custom_call" | custom-call | tf_op jit(solution)/shard_map/pallas_call | solution.py:275
  (32 shorter events, 0.6 us)
Async XLA Ops:
  0.6 8.9 %copy-start = (bf16[96,1024]{1,0:T(8,128)(2,1)S(1)}, bf16[96,1024]{1,0:T(8,128)(2,1)}, u32[]{:S(2)}) copy-start(bf16[96,1024]{1,0:T(8,128)(2,1)} %param.8) | copy-start | bytes 589828
  7.2 4.1 %copy-start.1 = (bf16[56,1024]{1,0:T(8,128)(2,1)S(1)}, bf16[56,1024]{1,0:T(8,128)(2,1)}, u32[]{:S(2)}) copy-start(bf16[56,1024]{1,0:T(8,128)(2,1)} %param.14) | copy-start | bytes 344068
  9.7 2.6 %copy-start.2 = (s32[16,56]{1,0:T(8,128)S(1)}, s32[16,56]{1,0:T(8,128)}, u32[]{:S(2)}) copy-start(s32[16,56]{1,0:T(8,128)} %param.12) | copy-start | bytes 10756

commit v5 on v4

--- a/solution.py
+++ b/solution.py
@@ -29,12 +29,22 @@
 MESH = pl.DeviceIdType.MESH
 
 
+PIECES = 3
+
+
+def piece_rows(rows, count):
+    halves = max(2, 2 * (count // 4 - 1))
+    cut = rows * (halves - 1) // halves // 16 * 16
+    size = -(-cut // (PIECES * 16)) * 16
+    return [(at, min(size, cut - at)) for at in range(0, cut, size)] + [(cut, rows - cut)]
+
+
 def spread_kernel(count, block_ref, all_ref, send_sem, recv_sem, own_sem):
     rows = block_ref.shape[0]
     length = count // 4
-    halves = max(2, 2 * (length - 1))
-    cut = rows * (halves - 1) // halves // 16 * 16
-    parts = (pl.ds(0, cut), pl.ds(cut, rows - cut))
+    parts = [pl.ds(*piece) for piece in piece_rows(rows, count)]
+    last = len(parts) - 1
+    lined = range(last)
     me = lax.axis_index("seq")
     at = me // 4
     inner = lax.rem(me, 4)
@@ -78,22 +88,28 @@
     local.start()
 
     def send_own(act):
-        act(1, me, 2, across, True)
-        pl.when(has_up)(lambda: act(0, me, 0, up, True))
-        pl.when(has_down)(lambda: act(0, me, 1, down, True))
-        pl.when(has_up)(lambda: act(1, me, 0, up, True))
-        pl.when(has_down)(lambda: act(1, me, 1, down, True))
-        act(0, me, 2, across, True)
-        act(1, me, 3, sibling, True)
-        act(0, me, 3, sibling, True)
+        act(last, me, 2, across, True)
+        for part in lined:
+            pl.when(has_up)(lambda part=part: act(part, me, 0, up, True))
+            pl.when(has_down)(lambda part=part: act(part, me, 1, down, True))
+        pl.when(has_up)(lambda: act(last, me, 0, up, True))
+        pl.when(has_down)(lambda: act(last, me, 1, down, True))
+        for part in lined:
+            act(part, me, 2, across, True)
+        for part in (last, *lined):
+            act(part, me, 3, sibling, True)
 
     def pass_across_first(act):
-        pl.when(has_up)(lambda: act(1, across, 0, up))
-        pl.when(has_down)(lambda: act(1, across, 1, down))
-        act(1, across, 3, sibling)
+        pl.when(has_up)(lambda: act(last, across, 0, up))
+        pl.when(has_down)(lambda: act(last, across, 1, down))
+        act(last, across, 3, sibling)
 
     def each(step, act, wait):
-        for part, where, cross in ((0, inner, True), (1, inner, False), (1, across_inner, False)):
+        for part, where, cross in (
+            *((part, inner, True) for part in lined),
+            (last, inner, False),
+            (last, across_inner, False),
+        ):
             for way, exists, more, device, place in (
                 (0, at - step >= 0, has_up, up, at - step),
                 (1, at + step < length, has_down, down, at + step),
@@ -115,17 +131,19 @@
             @pl.when(exists)
             def _(place=place):
                 block = place * 4 + across_inner
-                if wait:
-                    arrive(0, block)
-                act(0, block, 3, sibling)
+                for part in lined:
+                    if wait:
+                        arrive(part, block)
+                    act(part, block, 3, sibling)
 
     def crossed_here(act, wait):
-        if wait:
-            arrive(0, across)
-        act(0, across, 3, sibling)
+        for part in lined:
+            if wait:
+                arrive(part, across)
+            act(part, across, 3, sibling)
 
     send_own(begin)
-    arrive(1, across)
+    arrive(last, across)
     pass_across_first(begin)
 
     @pl.loop(1, length)
@@ -143,8 +161,8 @@
     def _(place):
         for other in range(2):
             block = place * 4 + other * 2 + lax.rem(core + 1, 2)
-            arrive(0, block)
-            arrive(1, block)
+            for part in range(last + 1):
+                arrive(part, block)
 
     def settle(part, block, way, device, own=False):
         copy(part, block, way, device, own).wait_send()
@@ -169,8 +187,8 @@
         in_specs=[pl.BlockSpec(memory_space=pltpu.VMEM)],
         out_specs=pl.BlockSpec(memory_space=pl.ANY),
         scratch_shapes=[
-            pltpu.SemaphoreType.DMA((4, 2, count)),
-            pltpu.SemaphoreType.DMA((2, count)),
+            pltpu.SemaphoreType.DMA((4, len(piece_rows(rows, count)), count)),
+            pltpu.SemaphoreType.DMA((len(piece_rows(rows, count)), count)),
             pltpu.SemaphoreType.DMA,
         ],
         compiler_params=pltpu.CompilerParams(collective_id=0, has_side_effects=True),

time: 63.8 us -> 63.7 us (level)
  no operation moved by 1% of the time
where the time goes in v5:
time: 63.7 us; the launch traced here: 63.2 us
  Pallas kernels  46.9 us (74%)
  other arithmetic  8.17 us (13%)
  local copies, waits for them, and re-layouts  4.29 us (7%)
  matrix products  3.01 us (5%)
  between operations  0.85 us (1%)
    pallas_call x1, Pallas kernels, spread(): pl.pallas_call(lambda *refs: spread_kernel(count, *refs), out_shape=jax.S...  30.6 us
    pallas_call x1, Pallas kernels, blend(): pl.pallas_call(blend_kernel, grid=(steps,), out_shape=(jax.ShapeDtypeStru...  16.3 us
    dot_general x3, matrix products, pick(): jnp.dot(one_hot.astype(jnp.float32), table, precision=lax.Precision.HIGHEST)  3.01 us
    convert_element_type x1, other arithmetic, shards(): start_angles = passage_start.astype(jnp.float32)[:, None] * frequency  1.37 us

profile of v5, /device:TPU:0, one launch (start us, length us, event | category | flops | bytes accessed | tf_op | source)
XLA Modules:
  0.0 63.2 jit_solution(3653543393894005211)
XLA Ops:
  0.7 1.0 %select_reduce_fusion = s32[96]{0:T(128)S(1)} fusion(s32[1536]{0:T(1024)} %param.13, s32[96]{0:T(128)S(1)} %iota_add_fusion.1), kind=kLoop, calls=%fused_computation.1 | loop fusion | flops 442272 | bytes 6912 | tf_op jit(solution)/shard_map/reduce_sum | solution.py:400
  1.6 0.9 %select_reduce_fusion.3 = s32[16]{0:T(128)S(1)} fusion(s32[16]{0:T(128)} %param.9, s32[16]{0:T(128)} %param.10), kind=kLoop, calls=%fused_computation.68 | loop fusion | flops 752 | bytes 192 | tf_op jit(solution)/shard_map/reduce_sum | solution.py:367
  2.6 1.4 %fusion.41 = (f32[16]{0:T(128)S(1)}, s32[]{:T(128)}) fusion(s32[16]{0:T(128)} %param.11, s32[]{:T(128)S(6)} %axis_index.12), kind=kLoop, calls=%fused_computation.99 | loop fusion | flops 63 | bytes 136 | tf_op jit(solution)/shard_map/convert_element_type | solution.py:370
  4.0 0.1 select_reduce_fusion.2
  4.2 0.8 %broadcast_add_fusion = (s32[16,56]{1,0:T(8,128)S(1)}, s32[56]{0:T(128)S(1)}) fusion(s32[16,56]{1,0:T(8,128)} %param.12, s32[16]{0:T(128)S(1)} %iota_multiply_fusion, pred[16]{0:T(512)(128)(4,1)S(1)} %iota_compare_fusion.3), kind=kLoop, calls=%fused_computation.75 | loop fusion | flops 2632 | bytes 7472 | tf_op jit(solution)/shard_map/add | solution.py:388
  5.0 0.6 %broadcast_add_fusion.1 = (s32[56]{0:T(128)S(1)}, f32[56]{0:T(128)S(1)}) fusion(s32[56]{0:T(128)S(1)} %get-tuple-element.11, s32[]{:T(128)S(6)} %mul.235, s32[]{:T(128)} %get-tuple-element.23), kind=kLoop, calls=%fused_computation.97 | loop fusion | flops 168 | bytes 680 | tf_op jit(solution)/shard_map/add | solution.py:429
  5.7 0.1 fusion.6
  5.9 0.1 multiply_cosine_fusion.1
  6.1 0.9 %fusion.33 = f32[96,56]{0,1:T(8,128)S(1)} fusion(s32[16,56]{1,0:T(8,128)} %param.12, s32[96]{0:T(128)S(1)} %get-tuple-element.3), kind=kOutput, calls=%fused_computation.65 | convolution fusion | flops 1034624 | bytes 25472 | tf_op jit(solution)/shard_map/dot_general | solution.py:330
  7.0 0.1 select_reduce_fusion.1
  7.1 0.1 copy.26
  7.2 0.8 %slice_convert_fusion = (f32[56,128]{1,0:T(8,128)S(1)}, bf16[56,128]{1,0:T(8,128)(2,1)S(1)}) fusion(bf16[56,256]{1,0:T(8,128)(2,1)} %param.15), kind=kLoop, calls=%fused_computation.48 | loop fusion | flops 7168 | bytes 71680 | tf_op jit(solution)/shard_map/convert_element_type | solution.py:355
  8.0 0.1 copy.29
  8.1 0.1 fusion.10
  8.2 0.1 add.297
  8.3 0.2 multiply_cosine_fusion
  8.5 0.1 copy.27
  8.6 0.8 %select_n.162.token_ref = s32[384,1]{1,0:T(8,128)} reshape(s32[96,4]{1,0:T(8,128)S(1)} %copy.29) | data formatting | bytes 3072 | tf_op jit(solution)/shard_map/jit(_where)/select_n | solution.py:420
  9.5 0.1 copy.28
  9.6 0.1 reshape.344
  9.7 0.8 %maximum_maximum_fusion.refs_0_ = bf16[448,256]{1,0:T(8,128)(2,1)} fusion(bf16[56,128]{1,0:T(8,128)(2,1)S(1)} %get-tuple-element.9, bf16[56,64]{1,0:T(8,128)(2,1)S(1)} %get-tuple-element.14, bf16[56,64]{1,0:T(8,128)(2,1)S(1)} %get-tuple-element.15, bf16[384,256]{1,0:T(8,128)(2,1)S(1)} %reshape.344, bf16[448]{0:T(512)(128)(2,1)S(1)} %pad.11.clone), kind=kLoop, calls=%fused_computation.2 | loop fusion | flops 1146880 | bytes 455552 | tf_op jit(solution)/shard_map/concatenate | solution.py:356
  10.5 0.8 %broadcast_in_dim_reshape.5.query_pos_ref = s32[448,1]{1,0:T(8,128)} reshape(s32[56,8]{1,0:T(8,128)S(1)} %broadcast_in_dim.133) | data formatting | bytes 3584 | tf_op jit(solution)/shard_map/broadcast_in_dim;reshape | solution.py:324
  11.4 0.1 fusion.4
  11.6 0.8 %pad_maximum_fusion.query_ref = bf16[448,128]{1,0:T(8,128)(2,1)} fusion(bf16[448,64]{1,0:T(8,128)(2,1)S(1)} %get-tuple-element.5, bf16[448,64]{1,0:T(8,128)(2,1)S(1)} %get-tuple-element.4), kind=kLoop, calls=%fused_computation.13 | loop fusion | flops 229376 | bytes 229376 | tf_op jit(solution)/shard_map/concatenate | solution.py:24
  12.3 0.3 fusion
  12.7 0.2 compare_reduce_fusion
  12.9 0.4 copy.25
  13.3 0.5 reduce_or.12
  13.8 0.7 %reshape.346.key_pos_ref = s32[4,1,1792]{2,1,0:T(1,128)} reshape(s32[16,448]{1,0:T(8,128)S(1)} %add_add_fusion) | data formatting | bytes 57344 | tf_op jit(solution)/shard_map/reshape | solution.py:322
  14.5 1.8 %fusion.2 = f32[1536,128]{1,0:T(8,128)} fusion(s32[1536]{0:T(1024)S(1)} %add_select_fusion.5, s32[16]{0:T(128)S(1)} %select_reduce_fusion.3, f32[16,64]{1,0:T(8,128)S(1)} %get-tuple-element.17, f32[16,64]{1,0:T(8,128)S(1)} %get-tuple-element.16), kind=kOutput, calls=%fused_computation.9 | convolution fusion | flops 37775360 | bytes 800832 | tf_op jit(solution)/shard_map/dot_general | solution.py:330
  16.3 30.6 %shard_map.95.all_ref = bf16[16,448,256]{2,1,0:T(8,128)(2,1)} custom-call(bf16[448,256]{1,0:T(8,128)(2,1)} %maximum_maximum_fusion.refs_0_), custom_call_target="tpu_custom_call" | custom-call | tf_op jit(solution)/shard_map/pallas_call | solution.py:184
  47.0 16.3 %shard_map.96 = (bf16[56,1024]{1,0:T(8,128)(2,1)}, bf16[96,1024]{1,0:T(8,128)(2,1)}) custom-call(bf16[16,448,256]{2,1,0:T(8,128)(2,1)} %shard_map.95.all_ref, f32[16,96,128]{2,1,0:T(8,128)} %bitcast.10, s32[4,1,1792]{2,1,0:T(1,128)} %reshape.346.key_pos_ref, bf16[448,128]{1,0:T(8,128)(2,1)} %pad_maximum_fusion.query_ref, ...), custom_call_target="tpu_custom_call" | custom-call | tf_op jit(solution)/shard_map/pallas_call | solution.py:293
  (32 shorter events, 0.6 us)
Async XLA Ops:
  0.6 8.9 %copy-start = (bf16[96,1024]{1,0:T(8,128)(2,1)S(1)}, bf16[96,1024]{1,0:T(8,128)(2,1)}, u32[]{:S(2)}) copy-start(bf16[96,1024]{1,0:T(8,128)(2,1)} %param.8) | copy-start | bytes 589828
  7.2 4.1 %copy-start.1 = (bf16[56,1024]{1,0:T(8,128)(2,1)S(1)}, bf16[56,1024]{1,0:T(8,128)(2,1)}, u32[]{:S(2)}) copy-start(bf16[56,1024]{1,0:T(8,128)(2,1)} %param.14) | copy-start | bytes 344068
  9.7 2.6 %copy-start.2 = (s32[16,56]{1,0:T(8,128)S(1)}, s32[16,56]{1,0:T(8,128)}, u32[]{:S(2)}) copy-start(s32[16,56]{1,0:T(8,128)} %param.12) | copy-start | bytes 10756

commit v6 on v5

--- a/solution.py
+++ b/solution.py
@@ -185,7 +185,7 @@
         lambda *refs: spread_kernel(count, *refs),
         out_shape=jax.ShapeDtypeStruct((count, rows, width), block.dtype),
         in_specs=[pl.BlockSpec(memory_space=pltpu.VMEM)],
-        out_specs=pl.BlockSpec(memory_space=pl.ANY),
+        out_specs=pl.BlockSpec(memory_space=pltpu.VMEM),
         scratch_shapes=[
             pltpu.SemaphoreType.DMA((4, len(piece_rows(rows, count)), count)),
             pltpu.SemaphoreType.DMA((len(piece_rows(rows, count)), count)),
@@ -220,18 +220,30 @@
     owner = lax.broadcasted_iota(jnp.int32, (unit, pages), 0) // PAGE
     expand = jnp.where(
         owner == lax.broadcasted_iota(jnp.int32, (unit, pages), 1), 1.0, 0.0
-    ).astype(jnp.float32)
+    ).astype(jnp.bfloat16)
+
+    def unfold(table):
+        high = table.astype(jnp.bfloat16)
+        rest = table - high.astype(jnp.float32)
+        middle = rest.astype(jnp.bfloat16)
+        low = (rest - middle.astype(jnp.float32)).astype(jnp.bfloat16)
+        thirds = jnp.dot(
+            expand,
+            jnp.concatenate([high, middle, low], axis=1),
+            preferred_element_type=jnp.float32,
+        )
+        return (
+            thirds[:, :head_dim]
+            + thirds[:, head_dim : 2 * head_dim]
+            + thirds[:, 2 * head_dim :]
+        )
+
     at_row = lax.broadcasted_iota(jnp.int32, (unit, head_dim), 0)
     at_lane = lax.broadcasted_iota(jnp.int32, (unit, head_dim), 1)
     still = jnp.where((at_row >= pages * PAGE) & (at_lane < half_dim), 1.0, 0.0)
     turn = jnp.concatenate(
         [
-            jnp.dot(
-                expand,
-                turn_ref[part],
-                precision=lax.Precision.HIGHEST,
-                preferred_element_type=jnp.float32,
-            )
+            unfold(turn_ref[part])
             + still
             for part in range(together)
         ],

time: 63.7 us -> 63.4 us (level)
    pallas_call x1, Pallas kernels: 16.3 us -> 14.7 us  [blend(): pl.pallas_call(blend_kernel, grid=(steps,), out_shape=(jax.ShapeDtypeStru...]
    pallas_call x1, Pallas kernels: 30.6 us -> 32 us  [spread(): pl.pallas_call(lambda *refs: spread_kernel(count, *refs), out_shape=jax.S...]
where the time goes in v6:
time: 63.4 us; the launch traced here: 62.9 us
  Pallas kernels  46.6 us (74%)
  other arithmetic  8.17 us (13%)
  local copies, waits for them, and re-layouts  4.29 us (7%)
  matrix products  3.01 us (5%)
  between operations  0.85 us (1%)
    pallas_call x1, Pallas kernels, spread(): pl.pallas_call(lambda *refs: spread_kernel(count, *refs), out_shape=jax.S...  32 us
    pallas_call x1, Pallas kernels, blend(): pl.pallas_call(blend_kernel, grid=(steps,), out_shape=(jax.ShapeDtypeStru...  14.7 us
    dot_general x3, matrix products, pick(): jnp.dot(one_hot.astype(jnp.float32), table, precision=lax.Precision.HIGHEST)  3.01 us
    convert_element_type x1, other arithmetic, shards(): start_angles = passage_start.astype(jnp.float32)[:, None] * frequency  1.37 us

profile of v6, /device:TPU:0, one launch (start us, length us, event | category | flops | bytes accessed | tf_op | source)
XLA Modules:
  0.0 62.9 jit_solution(14836050540145955375)
XLA Ops:
  0.7 1.0 %select_reduce_fusion = s32[96]{0:T(128)S(1)} fusion(s32[1536]{0:T(1024)} %param.13, s32[96]{0:T(128)S(1)} %iota_add_fusion.1), kind=kLoop, calls=%fused_computation.1 | loop fusion | flops 442272 | bytes 6912 | tf_op jit(solution)/shard_map/reduce_sum | solution.py:412
  1.6 0.9 %select_reduce_fusion.3 = s32[16]{0:T(128)S(1)} fusion(s32[16]{0:T(128)} %param.9, s32[16]{0:T(128)} %param.10), kind=kLoop, calls=%fused_computation.68 | loop fusion | flops 752 | bytes 192 | tf_op jit(solution)/shard_map/reduce_sum | solution.py:379
  2.6 1.4 %fusion.41 = (f32[16]{0:T(128)S(1)}, s32[]{:T(128)}) fusion(s32[16]{0:T(128)} %param.11, s32[]{:T(128)S(6)} %axis_index.12), kind=kLoop, calls=%fused_computation.99 | loop fusion | flops 63 | bytes 136 | tf_op jit(solution)/shard_map/convert_element_type | solution.py:382
  4.0 0.1 select_reduce_fusion.2
  4.2 0.8 %broadcast_add_fusion = (s32[16,56]{1,0:T(8,128)S(1)}, s32[56]{0:T(128)S(1)}) fusion(s32[16,56]{1,0:T(8,128)} %param.12, s32[16]{0:T(128)S(1)} %iota_multiply_fusion, pred[16]{0:T(512)(128)(4,1)S(1)} %iota_compare_fusion.3), kind=kLoop, calls=%fused_computation.75 | loop fusion | flops 2632 | bytes 7472 | tf_op jit(solution)/shard_map/add | solution.py:400
  5.0 0.6 %broadcast_add_fusion.1 = (s32[56]{0:T(128)S(1)}, f32[56]{0:T(128)S(1)}) fusion(s32[56]{0:T(128)S(1)} %get-tuple-element.11, s32[]{:T(128)S(6)} %mul.235, s32[]{:T(128)} %get-tuple-element.23), kind=kLoop, calls=%fused_computation.97 | loop fusion | flops 168 | bytes 680 | tf_op jit(solution)/shard_map/add | solution.py:441
  5.7 0.1 fusion.6
  5.9 0.1 multiply_cosine_fusion.1
  6.1 0.9 %fusion.33 = f32[96,56]{0,1:T(8,128)S(1)} fusion(s32[16,56]{1,0:T(8,128)} %param.12, s32[96]{0:T(128)S(1)} %get-tuple-element.3), kind=kOutput, calls=%fused_computation.65 | convolution fusion | flops 1034624 | bytes 25472 | tf_op jit(solution)/shard_map/dot_general | solution.py:342
  7.0 0.1 select_reduce_fusion.1
  7.1 0.1 copy.26
  7.2 0.8 %slice_convert_fusion = (f32[56,128]{1,0:T(8,128)S(1)}, bf16[56,128]{1,0:T(8,128)(2,1)S(1)}) fusion(bf16[56,256]{1,0:T(8,128)(2,1)} %param.15), kind=kLoop, calls=%fused_computation.48 | loop fusion | flops 7168 | bytes 71680 | tf_op jit(solution)/shard_map/convert_element_type | solution.py:367
  8.0 0.1 copy.29
  8.1 0.1 fusion.10
  8.2 0.1 add.297
  8.3 0.2 multiply_cosine_fusion
  8.5 0.1 copy.27
  8.6 0.8 %select_n.162.token_ref = s32[384,1]{1,0:T(8,128)} reshape(s32[96,4]{1,0:T(8,128)S(1)} %copy.29) | data formatting | bytes 3072 | tf_op jit(solution)/shard_map/jit(_where)/select_n | solution.py:432
  9.5 0.1 copy.28
  9.6 0.1 reshape.344
  9.7 0.8 %maximum_maximum_fusion.refs_0_ = bf16[448,256]{1,0:T(8,128)(2,1)} fusion(bf16[56,128]{1,0:T(8,128)(2,1)S(1)} %get-tuple-element.9, bf16[56,64]{1,0:T(8,128)(2,1)S(1)} %get-tuple-element.14, bf16[56,64]{1,0:T(8,128)(2,1)S(1)} %get-tuple-element.15, bf16[384,256]{1,0:T(8,128)(2,1)S(1)} %reshape.344, bf16[448]{0:T(512)(128)(2,1)S(1)} %pad.11.clone), kind=kLoop, calls=%fused_computation.2 | loop fusion | flops 1146880 | bytes 455552 | tf_op jit(solution)/shard_map/concatenate | solution.py:368
  10.5 0.8 %broadcast_in_dim_reshape.5.query_pos_ref = s32[448,1]{1,0:T(8,128)} reshape(s32[56,8]{1,0:T(8,128)S(1)} %broadcast_in_dim.133) | data formatting | bytes 3584 | tf_op jit(solution)/shard_map/broadcast_in_dim;reshape | solution.py:336
  11.4 0.1 fusion.4
  11.6 0.8 %pad_maximum_fusion.query_ref = bf16[448,128]{1,0:T(8,128)(2,1)} fusion(bf16[448,64]{1,0:T(8,128)(2,1)S(1)} %get-tuple-element.5, bf16[448,64]{1,0:T(8,128)(2,1)S(1)} %get-tuple-element.4), kind=kLoop, calls=%fused_computation.13 | loop fusion | flops 229376 | bytes 229376 | tf_op jit(solution)/shard_map/concatenate | solution.py:24
  12.3 0.3 fusion
  12.7 0.2 compare_reduce_fusion
  12.9 0.4 copy.25
  13.3 0.5 reduce_or.12
  13.8 0.7 %reshape.346.key_pos_ref = s32[4,1,1792]{2,1,0:T(1,128)} reshape(s32[16,448]{1,0:T(8,128)S(1)} %add_add_fusion) | data formatting | bytes 57344 | tf_op jit(solution)/shard_map/reshape | solution.py:334
  14.5 1.8 %fusion.2 = f32[1536,128]{1,0:T(8,128)} fusion(s32[1536]{0:T(1024)S(1)} %add_select_fusion.5, s32[16]{0:T(128)S(1)} %select_reduce_fusion.3, f32[16,64]{1,0:T(8,128)S(1)} %get-tuple-element.17, f32[16,64]{1,0:T(8,128)S(1)} %get-tuple-element.16), kind=kOutput, calls=%fused_computation.9 | convolution fusion | flops 37775360 | bytes 800832 | tf_op jit(solution)/shard_map/dot_general | solution.py:342
  16.3 32.0 %shard_map.95.all_ref = bf16[16,448,256]{2,1,0:T(8,128)(2,1)} custom-call(bf16[448,256]{1,0:T(8,128)(2,1)} %maximum_maximum_fusion.refs_0_), custom_call_target="tpu_custom_call" | custom-call | tf_op jit(solution)/shard_map/pallas_call | solution.py:184
  48.3 14.7 %shard_map.96 = (bf16[56,1024]{1,0:T(8,128)(2,1)}, bf16[96,1024]{1,0:T(8,128)(2,1)}) custom-call(bf16[16,448,256]{2,1,0:T(8,128)(2,1)} %shard_map.95.all_ref, f32[16,96,128]{2,1,0:T(8,128)} %bitcast.10, s32[4,1,1792]{2,1,0:T(1,128)} %reshape.346.key_pos_ref, bf16[448,128]{1,0:T(8,128)(2,1)} %pad_maximum_fusion.query_ref, ...), custom_call_target="tpu_custom_call" | custom-call | tf_op jit(solution)/shard_map/pallas_call | solution.py:305
  (32 shorter events, 0.6 us)
Async XLA Ops:
  0.6 8.9 %copy-start = (bf16[96,1024]{1,0:T(8,128)(2,1)S(1)}, bf16[96,1024]{1,0:T(8,128)(2,1)}, u32[]{:S(2)}) copy-start(bf16[96,1024]{1,0:T(8,128)(2,1)} %param.8) | copy-start | bytes 589828
  7.2 4.1 %copy-start.1 = (bf16[56,1024]{1,0:T(8,128)(2,1)S(1)}, bf16[56,1024]{1,0:T(8,128)(2,1)}, u32[]{:S(2)}) copy-start(bf16[56,1024]{1,0:T(8,128)(2,1)} %param.14) | copy-start | bytes 344068
  9.7 2.6 %copy-start.2 = (s32[16,56]{1,0:T(8,128)S(1)}, s32[16,56]{1,0:T(8,128)}, u32[]{:S(2)}) copy-start(s32[16,56]{1,0:T(8,128)} %param.12) | copy-start | bytes 10756

commit v7 on v6

--- a/solution.py
+++ b/solution.py
@@ -185,7 +185,7 @@
         lambda *refs: spread_kernel(count, *refs),
         out_shape=jax.ShapeDtypeStruct((count, rows, width), block.dtype),
         in_specs=[pl.BlockSpec(memory_space=pltpu.VMEM)],
-        out_specs=pl.BlockSpec(memory_space=pltpu.VMEM),
+        out_specs=pl.BlockSpec(memory_space=pl.ANY),
         scratch_shapes=[
             pltpu.SemaphoreType.DMA((4, len(piece_rows(rows, count)), count)),
             pltpu.SemaphoreType.DMA((len(piece_rows(rows, count)), count)),

time: 63.4 us -> 62.1 us (0.979)
  Pallas kernels: 46.6 us -> 45.3 us
    pallas_call x1, Pallas kernels: 32 us -> 30.6 us  [spread(): pl.pallas_call(lambda *refs: spread_kernel(count, *refs), out_shape=jax.S...]
where the time goes in v7:
time: 62.1 us; the launch traced here: 61.6 us
  Pallas kernels  45.3 us (73%)
  other arithmetic  8.17 us (13%)
  local copies, waits for them, and re-layouts  4.29 us (7%)
  matrix products  3.01 us (5%)
  between operations  0.85 us (1%)
    pallas_call x1, Pallas kernels, spread(): pl.pallas_call(lambda *refs: spread_kernel(count, *refs), out_shape=jax.S...  30.6 us
    pallas_call x1, Pallas kernels, blend(): pl.pallas_call(blend_kernel, grid=(steps,), out_shape=(jax.ShapeDtypeStru...  14.7 us
    dot_general x3, matrix products, pick(): jnp.dot(one_hot.astype(jnp.float32), table, precision=lax.Precision.HIGHEST)  3.01 us
    convert_element_type x1, other arithmetic, shards(): start_angles = passage_start.astype(jnp.float32)[:, None] * frequency  1.37 us

profile of v7, /device:TPU:0, one launch (start us, length us, event | category | flops | bytes accessed | tf_op | source)
XLA Modules:
  0.0 61.6 jit_solution(10457366061192565952)
XLA Ops:
  0.7 1.0 %select_reduce_fusion = s32[96]{0:T(128)S(1)} fusion(s32[1536]{0:T(1024)} %param.13, s32[96]{0:T(128)S(1)} %iota_add_fusion.1), kind=kLoop, calls=%fused_computation.1 | loop fusion | flops 442272 | bytes 6912 | tf_op jit(solution)/shard_map/reduce_sum | solution.py:412
  1.6 0.9 %select_reduce_fusion.3 = s32[16]{0:T(128)S(1)} fusion(s32[16]{0:T(128)} %param.9, s32[16]{0:T(128)} %param.10), kind=kLoop, calls=%fused_computation.68 | loop fusion | flops 752 | bytes 192 | tf_op jit(solution)/shard_map/reduce_sum | solution.py:379
  2.6 1.4 %fusion.41 = (f32[16]{0:T(128)S(1)}, s32[]{:T(128)}) fusion(s32[16]{0:T(128)} %param.11, s32[]{:T(128)S(6)} %axis_index.12), kind=kLoop, calls=%fused_computation.99 | loop fusion | flops 63 | bytes 136 | tf_op jit(solution)/shard_map/convert_element_type | solution.py:382
  4.0 0.1 select_reduce_fusion.2
  4.2 0.8 %broadcast_add_fusion = (s32[16,56]{1,0:T(8,128)S(1)}, s32[56]{0:T(128)S(1)}) fusion(s32[16,56]{1,0:T(8,128)} %param.12, s32[16]{0:T(128)S(1)} %iota_multiply_fusion, pred[16]{0:T(512)(128)(4,1)S(1)} %iota_compare_fusion.3), kind=kLoop, calls=%fused_computation.75 | loop fusion | flops 2632 | bytes 7472 | tf_op jit(solution)/shard_map/add | solution.py:400
  5.0 0.6 %broadcast_add_fusion.1 = (s32[56]{0:T(128)S(1)}, f32[56]{0:T(128)S(1)}) fusion(s32[56]{0:T(128)S(1)} %get-tuple-element.11, s32[]{:T(128)S(6)} %mul.235, s32[]{:T(128)} %get-tuple-element.23), kind=kLoop, calls=%fused_computation.97 | loop fusion | flops 168 | bytes 680 | tf_op jit(solution)/shard_map/add | solution.py:441
  5.7 0.1 fusion.6
  5.9 0.1 multiply_cosine_fusion.1
  6.1 0.9 %fusion.33 = f32[96,56]{0,1:T(8,128)S(1)} fusion(s32[16,56]{1,0:T(8,128)} %param.12, s32[96]{0:T(128)S(1)} %get-tuple-element.3), kind=kOutput, calls=%fused_computation.65 | convolution fusion | flops 1034624 | bytes 25472 | tf_op jit(solution)/shard_map/dot_general | solution.py:342
  7.0 0.1 select_reduce_fusion.1
  7.1 0.1 copy.26
  7.2 0.8 %slice_convert_fusion = (f32[56,128]{1,0:T(8,128)S(1)}, bf16[56,128]{1,0:T(8,128)(2,1)S(1)}) fusion(bf16[56,256]{1,0:T(8,128)(2,1)} %param.15), kind=kLoop, calls=%fused_computation.48 | loop fusion | flops 7168 | bytes 71680 | tf_op jit(solution)/shard_map/convert_element_type | solution.py:367
  8.0 0.1 copy.29
  8.1 0.1 fusion.10
  8.2 0.1 add.297
  8.3 0.2 multiply_cosine_fusion
  8.5 0.1 copy.27
  8.6 0.8 %select_n.162.token_ref = s32[384,1]{1,0:T(8,128)} reshape(s32[96,4]{1,0:T(8,128)S(1)} %copy.29) | data formatting | bytes 3072 | tf_op jit(solution)/shard_map/jit(_where)/select_n | solution.py:432
  9.5 0.1 copy.28
  9.6 0.1 reshape.344
  9.7 0.8 %maximum_maximum_fusion.refs_0_ = bf16[448,256]{1,0:T(8,128)(2,1)} fusion(bf16[56,128]{1,0:T(8,128)(2,1)S(1)} %get-tuple-element.9, bf16[56,64]{1,0:T(8,128)(2,1)S(1)} %get-tuple-element.14, bf16[56,64]{1,0:T(8,128)(2,1)S(1)} %get-tuple-element.15, bf16[384,256]{1,0:T(8,128)(2,1)S(1)} %reshape.344, bf16[448]{0:T(512)(128)(2,1)S(1)} %pad.11.clone), kind=kLoop, calls=%fused_computation.2 | loop fusion | flops 1146880 | bytes 455552 | tf_op jit(solution)/shard_map/concatenate | solution.py:368
  10.5 0.8 %broadcast_in_dim_reshape.5.query_pos_ref = s32[448,1]{1,0:T(8,128)} reshape(s32[56,8]{1,0:T(8,128)S(1)} %broadcast_in_dim.133) | data formatting | bytes 3584 | tf_op jit(solution)/shard_map/broadcast_in_dim;reshape | solution.py:336
  11.4 0.1 fusion.4
  11.6 0.8 %pad_maximum_fusion.query_ref = bf16[448,128]{1,0:T(8,128)(2,1)} fusion(bf16[448,64]{1,0:T(8,128)(2,1)S(1)} %get-tuple-element.5, bf16[448,64]{1,0:T(8,128)(2,1)S(1)} %get-tuple-element.4), kind=kLoop, calls=%fused_computation.13 | loop fusion | flops 229376 | bytes 229376 | tf_op jit(solution)/shard_map/concatenate | solution.py:24
  12.3 0.3 fusion
  12.7 0.2 compare_reduce_fusion
  12.9 0.4 copy.25
  13.3 0.5 reduce_or.12
  13.8 0.7 %reshape.346.key_pos_ref = s32[4,1,1792]{2,1,0:T(1,128)} reshape(s32[16,448]{1,0:T(8,128)S(1)} %add_add_fusion) | data formatting | bytes 57344 | tf_op jit(solution)/shard_map/reshape | solution.py:334
  14.5 1.8 %fusion.2 = f32[1536,128]{1,0:T(8,128)} fusion(s32[1536]{0:T(1024)S(1)} %add_select_fusion.5, s32[16]{0:T(128)S(1)} %select_reduce_fusion.3, f32[16,64]{1,0:T(8,128)S(1)} %get-tuple-element.17, f32[16,64]{1,0:T(8,128)S(1)} %get-tuple-element.16), kind=kOutput, calls=%fused_computation.9 | convolution fusion | flops 37775360 | bytes 800832 | tf_op jit(solution)/shard_map/dot_general | solution.py:342
  16.3 30.6 %shard_map.95.all_ref = bf16[16,448,256]{2,1,0:T(8,128)(2,1)} custom-call(bf16[448,256]{1,0:T(8,128)(2,1)} %maximum_maximum_fusion.refs_0_), custom_call_target="tpu_custom_call" | custom-call | tf_op jit(solution)/shard_map/pallas_call | solution.py:184
  47.0 14.7 %shard_map.96 = (bf16[56,1024]{1,0:T(8,128)(2,1)}, bf16[96,1024]{1,0:T(8,128)(2,1)}) custom-call(bf16[16,448,256]{2,1,0:T(8,128)(2,1)} %shard_map.95.all_ref, f32[16,96,128]{2,1,0:T(8,128)} %bitcast.10, s32[4,1,1792]{2,1,0:T(1,128)} %reshape.346.key_pos_ref, bf16[448,128]{1,0:T(8,128)(2,1)} %pad_maximum_fusion.query_ref, ...), custom_call_target="tpu_custom_call" | custom-call | tf_op jit(solution)/shard_map/pallas_call | solution.py:305
  (32 shorter events, 0.6 us)
Async XLA Ops:
  0.6 8.9 %copy-start = (bf16[96,1024]{1,0:T(8,128)(2,1)S(1)}, bf16[96,1024]{1,0:T(8,128)(2,1)}, u32[]{:S(2)}) copy-start(bf16[96,1024]{1,0:T(8,128)(2,1)} %param.8) | copy-start | bytes 589828
  7.2 4.1 %copy-start.1 = (bf16[56,1024]{1,0:T(8,128)(2,1)S(1)}, bf16[56,1024]{1,0:T(8,128)(2,1)}, u32[]{:S(2)}) copy-start(bf16[56,1024]{1,0:T(8,128)(2,1)} %param.14) | copy-start | bytes 344068
  9.7 2.6 %copy-start.2 = (s32[16,56]{1,0:T(8,128)S(1)}, s32[16,56]{1,0:T(8,128)}, u32[]{:S(2)}) copy-start(s32[16,56]{1,0:T(8,128)} %param.12) | copy-start | bytes 10756
